TPU v7x, 32 devices: a whole 2x2x4 slice. The times are simulated.
32 devices in a mesh: fsdp: 16 (over z, x, core), grp: 2 (over y).
Axes of the slice: x: 2, y: 2, z: 4, core: 2. Of those that a mesh axis runs over, the one named last changes fastest.
Arguments:
- block_in: bfloat16 [32, 680, 1024], P(('fsdp', 'grp')), may hold values from -6 to 6
- cotangent: bfloat16 [32, 680, 1024], P(('fsdp', 'grp')), may hold values from -6 to 6
- stop_scale: int32 [32], P(('fsdp', 'grp')), may hold values from 6 to 10
- class_label: int32 [32], P(('fsdp', 'grp')), may hold values from 0 to 999
- w_qkv: float32 [1024, 3072], P(('fsdp', 'grp')), may hold values from -0.1875 to 0.1875
- w_proj: float32 [1024, 1024], P(('fsdp', 'grp')), may hold values from -0.75 to 0.75
- w_fc1: float32 [1024, 4096], P(('fsdp', 'grp')), may hold values from -0.1875 to 0.1875
- w_fc2: float32 [4096, 1024], P(('fsdp', 'grp')), may hold values from -0.09375 to 0.09375
- w_ada: float32 [1024, 6144], P(('fsdp', 'grp')), may hold values from -0.1875 to 0.1875
- w_table: float32 [1000, 1024], P(None, ('fsdp', 'grp')), may hold values from -6 to 6
- m_qkv: float32 [1024, 3072], P(('fsdp', 'grp')), may hold values from -320 to 320
- m_proj: float32 [1024, 1024], P(('fsdp', 'grp')), may hold values from -96 to 96
- m_fc1: float32 [1024, 4096], P(('fsdp', 'grp')), may hold values from -256 to 256
- m_fc2: float32 [4096, 1024], P(('fsdp', 'grp')), may hold values from -256 to 256
- m_ada: float32 [1024, 6144], P(('fsdp', 'grp')), may hold values from -384 to 384
- m_table: float32 [1000, 1024], P(None, ('fsdp', 'grp')), may hold values from -80 to 80
- v_qkv: float32 [1024, 3072], P(('fsdp', 'grp')), may hold values from 2720 to 10880
- v_proj: float32 [1024, 1024], P(('fsdp', 'grp')), may hold values from 244.8 to 979.2
- v_fc1: float32 [1024, 4096], P(('fsdp', 'grp')), may hold values from 1740.8 to 6963.2
- v_fc2: float32 [4096, 1024], P(('fsdp', 'grp')), may hold values from 1740.8 to 6963.2
- v_ada: float32 [1024, 6144], P(('fsdp', 'grp')), may hold values from 3916.8 to 15667.2
- v_table: float32 [1000, 1024], P(None, ('fsdp', 'grp')), may hold values from 170 to 680
Outputs:
- block_out: bfloat16 [32, 680, 1024], P(('fsdp', 'grp'))
- grad_in: float32 [32, 680, 1024], P(('fsdp', 'grp'))
- new_qkv: float32 [1024, 3072], P(('fsdp', 'grp'))
- new_proj: float32 [1024, 1024], P(('fsdp', 'grp'))
- new_fc1: float32 [1024, 4096], P(('fsdp', 'grp'))
- new_fc2: float32 [4096, 1024], P(('fsdp', 'grp'))
- new_ada: float32 [1024, 6144], P(('fsdp', 'grp'))
- new_table: float32 [1000, 1024], P(None, ('fsdp', 'grp'))
- half_qkv: bfloat16 [1024, 3072], P(('fsdp', 'grp'))
- half_proj: bfloat16 [1024, 1024], P(('fsdp', 'grp'))
- half_fc1: bfloat16 [1024, 4096], P(('fsdp', 'grp'))
- half_fc2: bfloat16 [4096, 1024], P(('fsdp', 'grp'))
- half_ada: bfloat16 [1024, 6144], P(('fsdp', 'grp'))
- half_table: bfloat16 [1000, 1024], P(None, ('fsdp', 'grp'))
- first_qkv: float32 [1024, 3072], P(('fsdp', 'grp'))
- first_proj: float32 [1024, 1024], P(('fsdp', 'grp'))
- first_fc1: float32 [1024, 4096], P(('fsdp', 'grp'))
- first_fc2: float32 [4096, 1024], P(('fsdp', 'grp'))
- first_ada: float32 [1024, 6144], P(('fsdp', 'grp'))
- first_table: float32 [1000, 1024], P(None, ('fsdp', 'grp'))
- second_qkv: float32 [1024, 3072], P(('fsdp', 'grp'))
- second_proj: float32 [1024, 1024], P(('fsdp', 'grp'))
- second_fc1: float32 [1024, 4096], P(('fsdp', 'grp'))
- second_fc2: float32 [4096, 1024], P(('fsdp', 'grp'))
- second_ada: float32 [1024, 6144], P(('fsdp', 'grp'))
- second_table: float32 [1000, 1024], P(None, ('fsdp', 'grp'))
Inputs may be any that keep to these rules, and one draw needn't show every extreme that they name: An item holds the tokens of its first stop_scale scales, from the start of its 680 slots; later slots are padding.
All inputs are finite; a program needn't handle non-finite values.
Results may differ from a plain program's by a relative error of at most 0.017.
The roundings to bfloat16 on the way count: a program that leaves them out, or rounds other values in their place, can miss the bound.
Values may be sent and summed in bfloat16 or wider, within the bound.
No kernel may reach another device: no remote copies, remote signals or barrier semaphores. Data moves between devices by JAX's collectives and lax.ppermute only.
A program may use at most 256 MiB of HBM per device.

v0:
```python
import functools

import jax
import jax.numpy as jnp
import numpy as np
from jax import lax
from jax.experimental import pallas as pl
from jax.experimental.pallas import tpu as pltpu
from jax.sharding import PartitionSpec as P

D = 1024
HEADS = 16
HEAD = 64
FF = 4096
SCALES = 10
STEP = 3
AXES = ("fsdp", "grp")

patch_sides = (1, 2, 3, 4, 5, 6, 8, 10, 13, 16)
norm_eps = 1e-06
adam_eps = 1e-08
decay = 0.05
highest = lax.Precision.HIGHEST
bf16 = jnp.bfloat16
f32 = jnp.float32


def scale_layout(slots):
    squares = np.array(patch_sides[:SCALES], dtype=np.int64) ** 2
    bounds = np.cumsum(squares)
    scale_ids = np.searchsorted(bounds, np.arange(slots), side="right")
    return (bounds.astype(np.int32), scale_ids.astype(np.int32))


def norm_rows(values):
    centre = values - jnp.mean(values, axis=-1, keepdims=True)
    spread = jnp.mean(centre * centre, axis=-1, keepdims=True)
    return centre * lax.rsqrt(spread + norm_eps)


def modulate(values, scale_row, shift_row):
    return norm_rows(values) * (1.0 + scale_row) + shift_row


def gelu_tanh(values):
    return jax.nn.gelu(values, approximate=True)


def gelu_and_slope(v):
    root = np.float32(np.sqrt(2 / np.pi))
    cube = np.float32(0.044715) * root
    square = v * v
    t = jnp.tanh(v * (root + cube * square))
    half = 0.5 + 0.5 * t
    act = v * half
    return [half + act * ((1.0 - t) * (root + (3 * cube) * square)), act]


def learn_rates():
    return (D ** (-0.5), (D // 16) ** (-0.5), D ** (-0.5), FF ** (-0.5), D ** (-0.5), 1.0)


def adamw(weight, gradient, first, second, bias_one, bias_two, rate):
    first_new = 0.5 * first + 0.5 * gradient
    second_new = 0.5 * second + 0.5 * gradient * gradient
    update = first_new / bias_one / (jnp.sqrt(second_new / bias_two) + adam_eps) + decay * weight
    weight_new = weight - rate * update
    return (weight_new, weight_new.astype(bf16), first_new, second_new)


def contract_rows(former, latter):
    return lax.dot_general(former, latter, (((0,), (0,)), ((), ())), preferred_element_type=f32)


def contract_cols(former, latter):
    return lax.dot_general(former, latter, (((1,), (1,)), ((), ())), preferred_element_type=f32)


def dot_nt(former, latter):
    return lax.dot_general(former, latter, (((1,), (1,)), ((), ())), preferred_element_type=f32)


def dot_nn(former, latter):
    return lax.dot_general(former, latter, (((1,), (0,)), ((), ())), preferred_element_type=f32)


def dot_tn(former, latter):
    return lax.dot_general(former, latter, (((0,), (0,)), ((), ())), preferred_element_type=f32)


FORWARD_TILES = ((0, 240, 256), (240, 416, 432), (416, 680, 680))
BACKWARD_TILES = ((0, 128, 160), (128, 384, 432), (384, 680, 680))


def attend_kernel(q_ref, k_ref, v_ref, bias_ref, context_ref, lse_ref):
    for begin, end, keys in FORWARD_TILES:
        q = q_ref[begin:end, :] * bf16(0.125)
        lane = lax.broadcasted_iota(jnp.int32, q.shape, 1)
        contexts, totals = [], []
        for head in range(2):
            own = jnp.where((lane < HEAD) == (head == 0), q, bf16(0))
            scores = dot_nt(own, k_ref[:keys, :]) + bias_ref[begin:end, :keys]
            largest = jnp.max(scores, axis=1, keepdims=True)
            expo = jnp.exp(scores - largest)
            total = jnp.sum(expo, axis=1, keepdims=True)
            probs = (expo * (1.0 / total)).astype(bf16)
            totals.append(largest + jnp.log(total))
            contexts.append(dot_nn(probs, v_ref[:keys, :]))
        left = lax.broadcasted_iota(jnp.int32, contexts[0].shape, 1) < HEAD
        context_ref[begin:end, :] = jnp.where(left, contexts[0], contexts[1]).astype(bf16)
        lse = jnp.where(left, totals[0], totals[1]).T
        lse_ref[0, 0:1, begin:end] = lse[0:1]
        lse_ref[0, 1:2, begin:end] = lse[HEAD : HEAD + 1]


def attend_forward(packed, bias, begin, end, so_far=None):
    slots, width = packed.shape[0], packed.shape[1] // 3
    pairs = width // 128
    assert slots == FORWARD_TILES[-1][1]

    def block(offset):
        return pl.BlockSpec((slots, 128), lambda i: (0, offset + begin + i))

    more = list(so_far) if so_far else []

    def kernel(q_ref, k_ref, v_ref, bias_ref, *refs):
        attend_kernel(q_ref, k_ref, v_ref, bias_ref, *refs[len(more) :])

    return pl.pallas_call(
        kernel,
        grid=(end - begin,),
        in_specs=[
            block(0),
            block(pairs),
            block(2 * pairs),
            pl.BlockSpec((slots, slots), lambda i: (0, 0), pipeline_mode=pl.Buffered(1)),
        ]
        + [pl.BlockSpec(memory_space=pl.ANY)] * len(more),
        out_specs=[block(0), pl.BlockSpec((1, 2, slots), lambda i: (begin + i, 0, 0))],
        out_shape=[
            jax.ShapeDtypeStruct((slots, width), bf16),
            jax.ShapeDtypeStruct((pairs, 2, slots), f32),
        ],
        input_output_aliases={4 + i: i for i in range(len(more))},
        cost_estimate=estimate(
            flops=5 * slots * slots * width,
            bytes_accessed=6 * slots * width,
            transcendentals=slots * slots * HEADS // 2,
        ),
        compiler_params=pltpu.CompilerParams(vmem_limit_bytes=20 << 20),
        name="attend",
    )(packed, packed, packed, bias, *more)


def attend_back_kernel(
    half, place_ref, q_ref, k_ref, v_ref, grad_ref, lse_ref, bias_ref, out_ref, give_ref, *refs
):
    keys_ref, values_ref, y_ref, out_sems, give_sems = refs
    step = pl.program_id(0)
    slot = lax.rem(step, 2)
    width = 2 * half * 128

    def copies(step, slot, run):
        pair = lax.rem(step + (1 - place_ref[2]) * half, 2 * half)
        for i in range(3):
            at = pl.multiple_of(i * width + pair * 128, 128)
            run(
                pltpu.make_async_copy(
                    y_ref.at[slot, i], out_ref.at[:, pl.ds(at, 128)], out_sems.at[slot, i]
                )
            )

        @pl.when(step < half)
        def _():
            for i in range(3):
                at = pl.multiple_of((i * half + step) * 128, 128)
                run(
                    pltpu.make_async_copy(
                        y_ref.at[slot, i], give_ref.at[:, pl.ds(at, 128)], give_sems.at[slot, i]
                    )
                )

    @pl.when(step >= 2)
    def _():
        copies(step - 2, slot, lambda copy: copy.wait())

    for count, (begin, end, keys) in enumerate(reversed(BACKWARD_TILES)):
        q = q_ref[begin:end, :] * bf16(0.125)
        grad = grad_ref[begin:end, :]
        k = k_ref[:keys, :]
        v = v_ref[:keys, :]
        left = lax.broadcasted_iota(jnp.int32, q.shape, 1) < HEAD
        d_q, d_k, d_v = [], [], []
        for head in range(2):
            own = left == (head == 0)
            scores = dot_nt(k, jnp.where(own, q, bf16(0))) + bias_ref[:keys, begin:end]
            probs = jnp.exp(scores - lse_ref[0, head : head + 1, begin:end])
            d_probs = dot_nt(v, jnp.where(own, grad, bf16(0)))
            inner = jnp.sum(probs * d_probs, axis=0, keepdims=True)
            d_scores = (probs * (d_probs - inner)).astype(bf16)
            d_v.append(dot_nn(probs.astype(bf16), grad))
            d_k.append(dot_nn(d_scores, q))
            d_q.append(dot_tn(d_scores, k))
        first = lax.broadcasted_iota(jnp.int32, d_k[0].shape, 1) < HEAD
        d_k = jnp.where(first, d_k[0], d_k[1])
        d_v = jnp.where(first, d_v[0], d_v[1])
        if count == 0:
            keys_ref[:keys, :] = d_k
            values_ref[:keys, :] = d_v
        else:
            keys_ref[:keys, :] += d_k
            values_ref[:keys, :] += d_v
        y_ref[slot, 0, begin:end, :] = (jnp.where(left, d_q[0], d_q[1]) * 0.125).astype(bf16)
    y_ref[slot, 1] = keys_ref[...].astype(bf16)
    y_ref[slot, 2] = values_ref[...].astype(bf16)
    copies(step, slot, lambda copy: copy.start())

    @pl.when(step == 2 * half - 1)
    def _():
        copies(step - 1, 1 - slot, lambda copy: copy.wait())
        copies(step, slot, lambda copy: copy.wait())


def attend_backward(place, packed, d_context, lse, bias_t):
    slots, width = packed.shape[0], packed.shape[1] // 3
    pairs = width // 128
    half = pairs // 2
    assert slots == BACKWARD_TILES[-1][1] and pairs >= 2

    def at(i, place):
        return lax.rem(i + (1 - place[2]) * half, pairs)

    def block(offset):
        return pl.BlockSpec((slots, 128), lambda i, place: (0, offset + at(i, place)))

    return pl.pallas_call(
        functools.partial(attend_back_kernel, half),
        grid_spec=pltpu.PrefetchScalarGridSpec(
            num_scalar_prefetch=1,
            grid=(pairs,),
            in_specs=[
                block(0),
                block(pairs),
                block(2 * pairs),
                block(0),
                pl.BlockSpec((1, 2, slots), lambda i, place: (at(i, place), 0, 0)),
                pl.BlockSpec((slots, slots), lambda i, place: (0, 0), pipeline_mode=pl.Buffered(1)),
            ],
            out_specs=[pl.BlockSpec(memory_space=pl.ANY)] * 2,
            scratch_shapes=[
                pltpu.VMEM((slots, 128), f32),
                pltpu.VMEM((slots, 128), f32),
                pltpu.VMEM((2, 3, slots, 128), bf16),
                pltpu.SemaphoreType.DMA((2, 3)),
                pltpu.SemaphoreType.DMA((2, 3)),
            ],
        ),
        out_shape=[
            jax.ShapeDtypeStruct((slots, 3 * width), bf16),
            jax.ShapeDtypeStruct((slots, 3 * width // 2), bf16),
        ],
        cost_estimate=estimate(
            flops=20 * slots * slots * width,
            bytes_accessed=16 * slots * width,
            transcendentals=slots * slots * HEADS,
        ),
        compiler_params=pltpu.CompilerParams(vmem_limit_bytes=28 << 20),
        name="attend_back",
    )(place, packed, packed, packed, d_context, lse, bias_t)


def start_pieces(place_ref, pieces, w_ref, sems, rows, left, half, color):
    z, x, c, y = [place_ref[i] for i in range(4)]
    for far in range(2):
        for core in range(2):
            piece = pieces[core * 4 + far * 2 + color]
            for near in range(2):
                step_x, step_y = (far, near) if color == 0 else (near, far)
                for step in range(4):
                    at = (z ^ FLIPS[step]) * 2 + (x ^ step_x)
                    at = (at * 2 + (c ^ core)) * 2 + (y ^ step_y)
                    at = pl.multiple_of(at * rows, rows)
                    pltpu.make_async_copy(
                        piece.at[near, step, :, pl.ds(left, half)],
                        w_ref.at[color, pl.ds(at, rows), :],
                        sems.at[color],
                    ).start()


def gather_kernel(layout, place_ref, x_ref, *refs):
    rows, left, half, chunk, gelu, keep = layout
    outs = 2 if gelu else 1
    pieces, refs = refs[:8], refs[8:]
    whole_ref, refs = (refs[0], refs[1:]) if keep else (None, refs)
    out_refs, w_ref, y_refs = refs[:outs], refs[outs], refs[outs + 1 : 2 * outs + 1]
    in_sems, whole_sems, out_sems = refs[2 * outs + 1 :]
    start = functools.partial(start_pieces, place_ref, pieces, w_ref, in_sems, rows, left, half)
    start(0)
    waits = []
    for color in range(2):
        own = w_ref.at[color]
        pltpu.make_async_copy(own, own, in_sems.at[color]).wait()
        if color == 0:
            start(1)
        if keep:
            copy = pltpu.make_async_copy(
                own, whole_ref.at[:, pl.ds(color * half, half)], whole_sems.at[color]
            )
            copy.start()
            waits.append(copy)
        def outs_of(at, run):
            for i in range(outs):
                run(
                    pltpu.make_async_copy(
                        y_refs[i].at[:, pl.ds(at, chunk)],
                        out_refs[i].at[:, pl.ds(at, chunk)],
                        out_sems.at[i, at // chunk],
                    )
                )

        def step(n, carry, color=color):
            begin = pl.multiple_of(n * chunk, chunk)
            at = pl.multiple_of(color * half + n * chunk, chunk)
            result = dot_nn(x_ref[...], w_ref[color, :, pl.ds(begin, chunk)])
            values = gelu_and_slope(result) if gelu else [result]
            for i, value in enumerate(values):
                y_refs[i][:, pl.ds(at, chunk)] = value.astype(y_refs[i].dtype)
            outs_of(at, lambda copy: copy.start())
            return carry

        lax.fori_loop(0, half // chunk, step, 0)
        for n in range(half // chunk):
            outs_of(color * half + n * chunk, lambda copy: waits.append(copy))
    for copy in waits:
        copy.wait()


def gather_dot(place, x, pieces, left, half, kinds, keep, name):
    rows = pieces[0].shape[2]
    whole, width = rows * 32, 2 * half
    slots = x.shape[0]
    chunk = min(512, half)
    anywhere = pl.BlockSpec(memory_space=pl.ANY)
    shapes = [jax.ShapeDtypeStruct((whole, width), bf16)] * keep
    shapes += [jax.ShapeDtypeStruct((slots, width), kind) for kind in kinds]
    return pl.pallas_call(
        functools.partial(gather_kernel, (rows, left, half, chunk, len(kinds) == 2, keep)),
        grid_spec=pltpu.PrefetchScalarGridSpec(
            num_scalar_prefetch=1,
            grid=(1,),
            in_specs=[pl.BlockSpec(x.shape, lambda i, place: (0, 0))] + [anywhere] * 8,
            out_specs=[anywhere] * len(shapes),
            scratch_shapes=[pltpu.VMEM((2, whole, half), bf16)]
            + [pltpu.VMEM((slots, width), kind) for kind in kinds]
            + [
                pltpu.SemaphoreType.DMA((2,)),
                pltpu.SemaphoreType.DMA((2,)),
                pltpu.SemaphoreType.DMA((len(kinds), width // chunk)),
            ],
        ),
        out_shape=shapes,
        cost_estimate=estimate(
            flops=3 * slots * whole * width,
            bytes_accessed=2 * whole * width + 4 * slots * width,
            transcendentals=0,
        ),
        compiler_params=pltpu.CompilerParams(vmem_limit_bytes=56 << 20),
        name=name,
    )(place, x, *pieces)


def modulate_back_kernel(steps, more, place_ref, x_ref, w_ref, rows_ref, *refs):
    value_hbm, add_hbm, refs = refs[0], refs[1], refs[2:]
    if more:
        attended_hbm, proj_hbm, refs = refs[0], refs[1], refs[2:]
        out_hbm, low_hbm, give_hbm, context_hbm, sums_ref, refs = *refs[:5], refs[5:]
        total_ref, value_ref, add_ref, attended_ref, proj_ref, low_ref, context_ref, sems = refs
    else:
        out_hbm, sums_ref, total_ref, value_ref, add_ref, sems = refs
    step = pl.program_id(0)
    pairs = [(value_hbm, value_ref), (add_hbm, add_ref)]
    if more:
        pairs += [(attended_hbm, attended_ref), (proj_hbm, proj_ref)]
    loads = [pltpu.make_async_copy(a, b, sems.at[i]) for i, (a, b) in enumerate(pairs)]
    part = dot_nt(x_ref[...], w_ref[...])

    for i, load in enumerate(loads):

        @pl.when(step == min(i, steps - 2))
        def _(load=load):
            load.start()

    @pl.when(step == 0)
    def _():
        total_ref[...] = part

    @pl.when(step > 0)
    def _():
        total_ref[...] += part

    @pl.when(step == steps - 1)
    def _():
        for load in loads:
            load.wait()
        slots, width = total_ref.shape
        gain = rows_ref[0:1, :]
        length = place_ref[4]

        def block(at, count, sums):
            value = value_ref[pl.ds(at, count), :].astype(f32)
            centre = value - jnp.mean(value, axis=1, keepdims=True)
            rate = lax.rsqrt(jnp.mean(centre * centre, axis=1, keepdims=True) + norm_eps)
            normal = centre * rate
            grad = total_ref[pl.ds(at, count), :]
            scaled = grad * gain
            inner = jnp.mean(scaled * normal, axis=1, keepdims=True)
            result = rate * (scaled - jnp.mean(scaled, axis=1, keepdims=True) - normal * inner)
            add = add_ref[pl.ds(at, count), :].astype(f32)
            sums = [
                sums[0] + jnp.sum(grad * normal, axis=0, keepdims=True),
                sums[1] + jnp.sum(grad, axis=0, keepdims=True),
            ] + sums[2:]
            if more:
                slot = at + lax.broadcasted_iota(jnp.int32, (count, 1), 0)
                add = add * (slot < length).astype(f32)
            result = add + result
            total_ref[pl.ds(at, count), :] = result
            if more:
                attended = attended_ref[pl.ds(at, count), :]
                sums[2] = sums[2] + jnp.sum(result * attended, axis=0, keepdims=True)
                low_ref[pl.ds(at, count), :] = (result * rows_ref[1:2, :]).astype(bf16)
            return sums

        count = 32
        whole = slots // count
        sums = [jnp.zeros((1, width), f32) for _ in range(3 if more else 2)]
        sums = lax.fori_loop(
            0, whole, lambda i, sums: block(pl.multiple_of(i * count, count), count, sums), sums
        )
        if slots % count:
            sums = block(whole * count, slots % count, sums)
        sums_ref[...] = jnp.concatenate(
            sums + [jnp.zeros((8 - len(sums), width), f32)], axis=0
        )
        stores = [pltpu.make_async_copy(total_ref, out_hbm, sems.at[4])]
        if more:
            half = width // 2
            other = pl.multiple_of((1 - place_ref[2]) * half, half)
            stores += [
                pltpu.make_async_copy(low_ref.at[:, pl.ds(other, half)], give_hbm, sems.at[5]),
                pltpu.make_async_copy(low_ref, low_hbm, sems.at[6]),
            ]
        for store in stores:
            store.start()
        if more:
            context_ref[...] = dot_nt(low_ref[...], proj_ref[...]).astype(bf16)
            stores.append(pltpu.make_async_copy(context_ref, context_hbm, sems.at[7]))
            stores[-1].start()
        for store in stores:
            store.wait()


def modulate_back(place, x, weight, rows, value, add, attended=None, proj=None):
    more = proj is not None
    slots, depth = x.shape
    width = weight.shape[0]
    chunk = 1024
    assert depth % chunk == 0
    anywhere = pl.BlockSpec(memory_space=pl.ANY)
    operands = [value, add] + ([attended, proj] if more else [])
    shapes = [jax.ShapeDtypeStruct((slots, width), f32)]
    scratch = [
        pltpu.VMEM((slots, width), f32),
        pltpu.VMEM((slots, width), value.dtype),
        pltpu.VMEM((slots, width), add.dtype),
    ]
    if more:
        shapes += [
            jax.ShapeDtypeStruct((slots, width), bf16),
            jax.ShapeDtypeStruct((slots, width // 2), bf16),
            jax.ShapeDtypeStruct((slots, width), bf16),
        ]
        scratch += [
            pltpu.VMEM((slots, width), f32),
            pltpu.VMEM(proj.shape, bf16),
            pltpu.VMEM((slots, width), bf16),
            pltpu.VMEM((slots, width), bf16),
        ]
    return pl.pallas_call(
        functools.partial(modulate_back_kernel, depth // chunk, more),
        grid_spec=pltpu.PrefetchScalarGridSpec(
            num_scalar_prefetch=1,
            grid=(depth // chunk,),
            in_specs=[
                pl.BlockSpec((slots, chunk), lambda i, place: (0, i)),
                pl.BlockSpec((width, chunk), lambda i, place: (0, i)),
                pl.BlockSpec((8, width), lambda i, place: (0, 0)),
            ]
            + [anywhere] * len(operands),
            out_specs=[anywhere] * len(shapes)
            + [pl.BlockSpec((8, width), lambda i, place: (0, 0))],
            scratch_shapes=scratch + [pltpu.SemaphoreType.DMA((8,))],
        ),
        out_shape=shapes + [jax.ShapeDtypeStruct((8, width), f32)],
        cost_estimate=estimate(
            flops=3 * slots * width * (depth + width * more),
            bytes_accessed=2 * (slots + width) * depth + 16 * slots * width,
            transcendentals=0,
        ),
        compiler_params=pltpu.CompilerParams(vmem_limit_bytes=48 << 20),
        name="modulate_back",
    )(place, x, weight, rows, *operands)


def gelu_back_kernel(rows, place_ref, grad_ref, slope_ref, *refs):
    pieces, (out_ref, give_ref), refs = refs[:8], refs[8:10], refs[10:]
    w_ref, s_ref, y_ref, in_sems, s_sems, y_sems, give_sems = refs
    z, x, c, y = [place_ref[i] for i in range(4)]
    block = 4 * rows
    chunks = [(step, far_x) for step in range(4) for far_x in range(2)]
    where = [
        pl.multiple_of(((z ^ FLIPS[step]) * 2 + (x ^ far_x)) * block, block) for step, far_x in chunks
    ]
    half = pieces[0].shape[-1]

    def start(n):
        step, far_x = chunks[n]
        for core in range(2):
            for far_y in range(2):
                at = pl.multiple_of(((c ^ core) * 2 + (y ^ far_y)) * rows, rows)
                for color in range(2):
                    far, near = (far_x, far_y) if color == 0 else (far_y, far_x)
                    pltpu.make_async_copy(
                        pieces[core * 4 + far * 2 + color].at[near, step],
                        w_ref.at[n, pl.ds(at, rows), pl.ds(color * half, half)],
                        in_sems.at[n],
                    ).start()
        pltpu.make_async_copy(
            slope_ref.at[:, pl.ds(where[n], block)], s_ref.at[n], s_sems.at[n]
        ).start()

    def give(n, run):
        @pl.when(lax.shift_right_logical(z ^ FLIPS[chunks[n][0]], 1) != c)
        def _():
            at = pl.multiple_of(where[n] - (1 - c) * (4 * block), block)
            run(
                pltpu.make_async_copy(
                    y_ref.at[n], give_ref.at[:, pl.ds(at, block)], give_sems.at[n]
                )
            )

    ahead = 2
    for n in range(ahead):
        start(n)
    waits = []
    for n in range(len(chunks)):
        pltpu.make_async_copy(w_ref.at[n], w_ref.at[n], in_sems.at[n]).wait()
        pltpu.make_async_copy(s_ref.at[n], s_ref.at[n], s_sems.at[n]).wait()
        if n + ahead < len(chunks):
            start(n + ahead)
        y_ref[n] = (dot_nt(grad_ref[...], w_ref[n]) * s_ref[n].astype(f32)).astype(bf16)
        copy = pltpu.make_async_copy(
            y_ref.at[n], out_ref.at[:, pl.ds(where[n], block)], y_sems.at[n]
        )
        copy.start()
        waits.append(copy)
        give(n, lambda copy: copy.start())
    for n in range(len(chunks)):
        give(n, lambda copy: copy.wait())
    for copy in waits:
        copy.wait()


def gelu_back_dot(place, grad, slope, pieces):
    slots, width = slope.shape
    rows = pieces[0].shape[2]
    assert width == 32 * rows and grad.shape[1] == 2 * pieces[0].shape[3]
    anywhere = pl.BlockSpec(memory_space=pl.ANY)
    block = 4 * rows
    return pl.pallas_call(
        functools.partial(gelu_back_kernel, rows),
        grid_spec=pltpu.PrefetchScalarGridSpec(
            num_scalar_prefetch=1,
            grid=(1,),
            in_specs=[pl.BlockSpec(grad.shape, lambda i, place: (0, 0))] + [anywhere] * 9,
            out_specs=[anywhere] * 2,
            scratch_shapes=[
                pltpu.VMEM((8, block, grad.shape[1]), bf16),
                pltpu.VMEM((8, slots, block), slope.dtype),
                pltpu.VMEM((8, slots, block), bf16),
            ]
            + [pltpu.SemaphoreType.DMA((8,))] * 4,
        ),
        out_shape=[
            jax.ShapeDtypeStruct((slots, width), bf16),
            jax.ShapeDtypeStruct((slots, width // 2), bf16),
        ],
        cost_estimate=estimate(
            flops=3 * slots * width * grad.shape[1],
            bytes_accessed=8 * slots * width + 4 * width * grad.shape[1],
            transcendentals=0,
        ),
        compiler_params=pltpu.CompilerParams(vmem_limit_bytes=56 << 20),
        name="gelu_back",
    )(place, grad, slope, *pieces)


def weight_grad_kernel(depth, rows, turn, firsts, place_ref, *refs):
    products = len(firsts)
    ins, out_refs = refs[: 4 * products], refs[4 * products :]
    step = pl.program_id(0)
    inner = lax.rem(step, turn)

    def product(own_ref, other_ref, mine_ref, take_ref):
        total = dot_tn(own_ref[...], mine_ref[...]) + dot_tn(other_ref[...], take_ref[...])
        total = total.reshape(depth, 2, 2, 2, rows, total.shape[-1])

        @pl.when(step < turn)
        def _():
            first = place_ref[3] == 0
            for x in range(2):
                low, high = total[:, x, :, 0], total[:, x, :, 1]
                out_refs[0][x] = jnp.where(first, high, low).astype(bf16)
                out_refs[1][x] = jnp.where(first, low, high).astype(bf16)

        @pl.when(step >= turn)
        def _():
            first = place_ref[1] == 0
            for y in range(2):
                low, high = total[:, 0, :, y], total[:, 1, :, y]
                out_refs[2][y] = jnp.where(first, high, low).astype(bf16)
                out_refs[3][y] = jnp.where(first, low, high).astype(bf16)

    if products == 1:
        product(*ins)
        return
    for n, (begin, end) in enumerate(firsts):

        @pl.when((inner >= begin) & (inner < end))
        def _(n=n):
            product(*ins[4 * n : 4 * n + 4])


def weight_grad_call(place, products, rows, chunk):
    specs, operands, firsts = [], [], []
    turn = flops = 0
    for own, other, rhs, take, groups in products:
        slots, columns = rhs.shape[0], rhs.shape[1] // groups
        per = columns // 2 // chunk
        count = groups * per // 2
        assert groups * per % 2 == 0 and columns % (2 * chunk) == 0
        flops += 6 * slots * own.shape[1] * groups * columns // 2
        firsts.append((turn, turn + count))
        specs.append((per, count, turn))
        turn += count
        operands += [own, other, rhs, take]
    in_specs = []
    for (own, *_), (per, count, begin) in zip(products, specs):
        slots = own.shape[0]

        def which(i, count=count, begin=begin):
            color = i // turn
            return color * count + jnp.clip(i - color * turn - begin, 0, count - 1)

        once = pl.Buffered(1)
        in_specs += [pl.BlockSpec(own.shape, lambda i, place: (0, 0), pipeline_mode=once)] * 2
        in_specs.append(
            pl.BlockSpec(
                (slots, chunk),
                lambda i, place, which=which, per=per: (
                    0,
                    (which(i) // per * 2 + place[2]) * per + lax.rem(which(i), per),
                ),
            )
        )
        in_specs.append(
            pl.BlockSpec((slots, chunk), lambda i, place, which=which: (0, which(i)))
        )
    width = products[0][0].shape[1]
    depth = width // rows // 8
    block = (2, depth, 2, rows, chunk)
    early = pl.BlockSpec(block, lambda i, place: (0, 0, 0, 0, jnp.minimum(i, turn - 1)))
    late = pl.BlockSpec(block, lambda i, place: (0, 0, 0, 0, jnp.maximum(i - turn, 0)))
    shape = jax.ShapeDtypeStruct((2, depth, 2, rows, turn * chunk), bf16)
    return pl.pallas_call(
        functools.partial(weight_grad_kernel, depth, rows, turn, tuple(firsts)),
        grid_spec=pltpu.PrefetchScalarGridSpec(
            num_scalar_prefetch=1,
            grid=(2 * turn,),
            in_specs=in_specs,
            out_specs=[early, early, late, late],
        ),
        out_shape=[shape] * 4,
        cost_estimate=estimate(
            flops=flops,
            bytes_accessed=sum(2 * v.size for v in operands) + 4 * width * turn * chunk,
            transcendentals=0,
        ),
        compiler_params=pltpu.CompilerParams(vmem_limit_bytes=60 << 20),
        name="weight_grad",
    )(place, *operands)


def estimate(flops, bytes_accessed, transcendentals):
    return pl.CostEstimate(
        flops=flops // 64, bytes_accessed=bytes_accessed // 64, transcendentals=transcendentals // 64
    )


def weight_grad_rows_kernel(rows, place_ref, own_ref, other_ref, mine_ref, take_ref, *out_refs):
    total = dot_tn(own_ref[...], mine_ref[...]) + dot_tn(other_ref[...], take_ref[...])
    total = total.reshape(2, 2, 2, rows, total.shape[-1])
    half = total.shape[-1] // 2
    first_y, first_x = place_ref[3] == 0, place_ref[1] == 0
    for i in range(2):
        low, high = total[i, :, 0, :, :half], total[i, :, 1, :, :half]
        out_refs[0][i, 0] = jnp.where(first_y, high, low).astype(bf16)
        out_refs[1][i, 0] = jnp.where(first_y, low, high).astype(bf16)
        low, high = total[0, :, i, :, half:], total[1, :, i, :, half:]
        out_refs[2][i, 0] = jnp.where(first_x, high, low).astype(bf16)
        out_refs[3][i, 0] = jnp.where(first_x, low, high).astype(bf16)


def weight_grad_rows(place, own, other, rhs, take, rows):
    slots, width = own.shape
    half = take.shape[1]
    depth = width // rows // 8
    out = pl.BlockSpec((2, 1, 2, rows, half // 2), lambda i, place: (0, i, 0, 0, 0))
    by_z = pl.BlockSpec((slots, 8 * rows), lambda i, place: (0, i))
    shape = jax.ShapeDtypeStruct((2, depth, 2, rows, half // 2), bf16)
    return pl.pallas_call(
        functools.partial(weight_grad_rows_kernel, rows),
        grid_spec=pltpu.PrefetchScalarGridSpec(
            num_scalar_prefetch=1,
            grid=(depth,),
            in_specs=[
                by_z,
                by_z,
                pl.BlockSpec((slots, half), lambda i, place: (0, place[2])),
                pl.BlockSpec((slots, half), lambda i, place: (0, 0)),
            ],
            out_specs=[out] * 4,
        ),
        out_shape=[shape] * 4,
        cost_estimate=estimate(
            flops=4 * slots * width * half,
            bytes_accessed=4 * slots * (width + half) + 2 * width * half,
            transcendentals=0,
        ),
        compiler_params=pltpu.CompilerParams(vmem_limit_bytes=60 << 20),
        name="weight_grad_rows",
    )(place, own, other, rhs, take)


class Line:
    def __init__(self):
        self.last = jnp.zeros((8, 128), f32)

    def __call__(self, *values):
        self.last, values = lax.optimization_barrier((self.last, values))
        return values[0] if len(values) == 1 else values

    def arrive(self, movers, *values):
        gots, values = self([mover.got for mover in movers], values)
        for mover, got in zip(movers, gots):
            mover.got = got
        return values[0] if len(values) == 1 else values


class Scatter:
    def __init__(self, grid, line, rows):
        self.grid, self.line, self.flips = grid, line, grid.bits()
        self.rows = rows.reshape([2] * len(self.flips) + list(rows.shape[1:]))

    def start(self):
        dim = len(self.flips) - 1
        axis, bit = self.flips.pop(0)
        self.own = lax.index_in_dim(self.rows, 0, dim, keepdims=False)
        away = self.line(lax.index_in_dim(self.rows, 1, dim, keepdims=False))
        self.got = self.grid.flip(away, axis, bit)

    def add(self):
        self.rows = self.own + self.got


class Gather:
    orders = ("yx", "xy")

    def __init__(self, grid, line, shards):
        self.grid, self.line = grid, line
        lows = [shard[:, : shard.shape[1] // 2] for shard in shards]
        highs = [shard[:, shard.shape[1] // 2 :] for shard in shards]
        self.shard = jnp.concatenate(lows + highs, axis=1)

    def first(self):
        self.shard = self.line(self.shard)
        self.got = self.grid.flip(self.shard, "z", 2)

    def second(self):
        self.pair = self.line(jnp.stack([self.shard, self.got]))
        self.got = self.grid.flip(self.pair, "z", 1)

    def third(self):
        half = self.shard.shape[1] // 2
        pairs = (self.pair, self.got)
        rows = [
            jnp.concatenate([p[:, :, i * half : (i + 1) * half] for p in pairs], axis=0)
            for i in range(2)
        ]
        self.rows = self.line(*rows)
        self.got = [self.grid.flip(v, o[0], 1) for v, o in zip(self.rows, self.orders)]

    def fourth(self):
        plane = [
            jnp.concatenate([own[None], new[None]], axis=0) for own, new in zip(self.rows, self.got)
        ]
        self.plane = self.line(*plane)
        self.got = [self.grid.flip(v, o[1], 1) for v, o in zip(self.plane, self.orders)]
        self.near = [self.grid.flip(v, "c", 1) for v in self.plane]

    def pieces(self):
        far = [self.grid.flip(v, "c", 1) for v in self.got]
        return list(self.plane) + list(self.got) + list(self.near) + far


FLIPS = (0, 2, 1, 3)


def add_split_kernel(joined, place_ref, *refs):
    sums = len(refs) // (5 if joined else 6)
    outs = refs[4 * sums :]
    for n in range(sums):
        for side in range(2):
            one, two = refs[4 * n + 2 * side], refs[4 * n + 2 * side + 1]
            out = outs[side] if joined else outs[2 * n + side]
            total = one[...].astype(f32) + two[...].astype(f32)
            if joined:
                width = total.shape[-1]
                out[..., n * width : (n + 1) * width] = total.astype(out.dtype)
            else:
                out[...] = total.reshape(out.shape).astype(out.dtype)


def add_split(place, name, steps, specs, *pairs, joined=False, kind=bf16):
    in_specs, operands, out_specs, shapes = [], [], [], []
    for n, pair in enumerate(pairs):
        lead = pair[0].ndim - 3
        if pair[0].ndim == 3:
            lead = 1
        tail = pair[0].shape[lead:]
        for side in range(2):
            for array in pair:
                in_specs.append(
                    pl.BlockSpec(
                        (1,) * lead + tail,
                        lambda i, place, n=n, side=side, zeros=(0,) * len(tail): (
                            specs(i, place)[n][side] + zeros
                        ),
                    )
                )
                operands.append(array)
            if joined and n:
                continue
            wide = tail[:-1] + (tail[-1] * (len(pairs) if joined else 1),)
            out_specs.append(
                pl.BlockSpec(
                    (1,) + wide, lambda i, place, zeros=(0,) * len(wide): (i,) + zeros
                )
            )
            shapes.append(jax.ShapeDtypeStruct((steps,) + wide, kind))
    return pl.pallas_call(
        functools.partial(add_split_kernel, joined),
        grid_spec=pltpu.PrefetchScalarGridSpec(
            num_scalar_prefetch=1, grid=(steps,), in_specs=in_specs, out_specs=out_specs
        ),
        out_shape=shapes,
        cost_estimate=estimate(
            flops=sum(array.size for array in operands),
            bytes_accessed=4 * sum(array.size for array in operands),
            transcendentals=0,
        ),
        compiler_params=pltpu.CompilerParams(vmem_limit_bytes=24 << 20),
        name=name,
    )(place, *operands)


class GradSum:
    def __init__(self, grid, line, here, place, products, rows, chunk, movers=()):
        self.grid, self.line, self.here, self.place, self.rows = grid, line, here, place, rows
        self.shapes = [(groups, rhs.shape[1] // groups) for _, _, rhs, _, groups in products]
        if len(products) == 1 and products[0][4] == 1:
            grads = weight_grad_rows(place, *products[0][:4], rows)
        else:
            grads = weight_grad_call(place, products, rows, chunk)
        away_one, self.one, away_two, self.two = line.arrive(movers, *grads)
        self.got = [grid.flip(away_one, "y", 1), grid.flip(away_two, "x", 1)]

    def second(self):
        away_one, self.one, away_two, self.two = self.line(
            *add_split(self.place, "add_second", 4, self.second_specs, *self.parts())
        )
        self.got = [self.grid.flip(away_one, "x", 1), self.grid.flip(away_two, "y", 1)]

    def parts(self):
        return [(self.one, self.got[0]), (self.two, self.got[1])]

    def second_specs(self, i, place):
        x, y = place[1], place[3]
        return [((1 - x, i), (x, i)), ((1 - y, i), (y, i))]

    def third(self):
        def specs(i, place):
            low = lax.rem(place[0], 2)
            pair = ((2 * i + 1 - low,), (2 * i + low,))
            return [pair, pair]

        away, self.both = self.line(
            *add_split(self.place, "add_third", 2, specs, *self.parts(), joined=True)
        )
        self.got = self.grid.flip(away, "z", 1)

    def fourth(self):
        def specs(i, place):
            high = place[0] // 2
            return [((1 - high,), (high,))]

        away, self.both = self.line(
            *add_split(self.place, "add_fourth", 1, specs, (self.both, self.got))
        )
        away, self.both = away[0], self.both[0]
        self.got = self.grid.flip(away, "z", 2)

    def fifth(self):
        def specs(i, place):
            return [((1 - place[2],), (place[2],))]

        give, self.keep = self.line(
            *add_split(self.place, "add_fifth", 1, specs, (self.both, self.got), kind=f32)
        )
        give, self.keep = give[0], self.keep[0]
        self.take = self.grid.flip(give, "c", 1)

    def result(self):
        first = self.here["c"] == 0
        low = jnp.where(first, self.keep, self.take)
        high = jnp.where(first, self.take, self.keep)
        sums, left, middle = [], 0, low.shape[1] // 2
        for groups, columns in self.shapes:
            part = groups * columns // 4
            half = columns // 2
            sides = []
            for side in (low, high):
                colors = [side[:, left : left + part], side[:, middle + left : middle + left + part]]
                sides.append(jnp.concatenate(colors, axis=1))
            spans = [side[:, g * half : (g + 1) * half] for g in range(groups) for side in sides]
            sums.append(jnp.concatenate(spans, axis=1))
            left += part
        return sums


class Grid:
    def __init__(self, fsdp, grp):
        outer = fsdp // 2
        self.size = {"c": 2, "x": 2 if outer % 2 == 0 else 1, "y": grp}
        self.size["z"] = outer // self.size["x"]
        self.count = fsdp * grp
        self.fsdp = fsdp

    def here(self):
        place = lax.axis_index("fsdp")
        wide = self.size["x"]
        return {
            "c": place % 2,
            "x": (place // 2) % wide,
            "z": place // (2 * wide),
            "y": lax.axis_index("grp"),
        }

    def shift(self, array, axis, step):
        size = self.size[axis]
        if axis == "y":
            return lax.ppermute(array, "grp", [(i, (i + step) % size) for i in range(size)])
        stride = {"c": 1, "x": 2, "z": 2 * self.size["x"]}[axis]
        pairs = []
        for i in range(self.fsdp):
            at = (i // stride) % size
            pairs.append((i, i + ((at + step) % size - at) * stride))
        return lax.ppermute(array, "fsdp", pairs)

    def fits(self, rows):
        size = self.size
        return size["x"] == 2 and size["y"] == 2 and size["z"] == 4 and rows % 32 == 0

    def bits(self):
        flips = []
        for axis in "cxyz":
            size = self.size[axis]
            assert size & (size - 1) == 0
            bit = size // 2
            while bit:
                flips.append((axis, bit))
                bit //= 2
        return flips

    def gather_all(self, row, flips):
        for axis, bit in flips:
            row = jnp.concatenate([row[None], self.flip(row, axis, bit)[None]], axis=0)
        return row

    def sources(self, here):
        flips = self.bits()
        turn = {axis: np.zeros(self.count, np.int32) for axis in "cxyz"}
        for n in range(self.count):
            for k, (axis, bit) in enumerate(flips):
                if n >> k & 1:
                    turn[axis][n] ^= bit
        z, x, c, y = [here[axis] ^ turn[axis] for axis in "zxcy"]
        return ((z * self.size["x"] + x) * 2 + c) * self.size["y"] + y

    def flip(self, array, axis, bit):
        size = self.size[axis]
        if axis == "y":
            return lax.ppermute(array, "grp", [(i, i ^ bit) for i in range(size)])
        stride = {"c": 1, "x": 2, "z": 2 * self.size["x"]}[axis]
        pairs = [
            (i, i + (((i // stride) % size ^ bit) - (i // stride) % size) * stride)
            for i in range(self.fsdp)
        ]
        return lax.ppermute(array, "fsdp", pairs)

    def scatter_sum(self, array, axis, dim, here, kind=bf16):
        size = self.size[axis]
        total = lax.dynamic_index_in_dim(array, here[axis], dim, keepdims=False)
        for step in range(1, size):
            piece = lax.dynamic_index_in_dim(array, (here[axis] + step) % size, dim, keepdims=False)
            total = total + self.shift(piece.astype(kind), axis, step).astype(f32)
        return total


def per_device(
    grid,
    block_in,
    cotangent,
    stop_scale,
    class_label,
    w_qkv,
    w_proj,
    w_fc1,
    w_fc2,
    w_ada,
    w_table,
    m_qkv,
    m_proj,
    m_fc1,
    m_fc2,
    m_ada,
    m_table,
    v_qkv,
    v_proj,
    v_fc1,
    v_fc2,
    v_ada,
    v_table,
):
    items, slots, width = block_in.shape
    assert items == 1
    here = grid.here()
    bounds, scale_ids = scale_layout(slots)
    picked = jnp.arange(SCALES) == stop_scale[0] - 1
    length = jnp.sum(jnp.where(picked, jnp.asarray(bounds), 0))
    position = jnp.arange(slots)
    valid = (position < length).astype(f32)[:, None]
    scale_table = jnp.asarray(scale_ids)

    def mask(length):
        allowed = (scale_table[None, :] <= scale_table[:, None]) & (position[None, :] < length)
        return jnp.where(allowed, f32(0), f32(-1e30))

    place = jnp.stack([here[axis] for axis in "zxcy"] + [length]).astype(jnp.int32)
    fits = grid.fits(w_qkv.shape[0])
    cast_qkv, cast_proj, cast_fc1, cast_fc2 = [
        w.astype(bf16) for w in (w_qkv, w_proj, w_fc1, w_fc2)
    ]
    half_qkv, half_proj, half_fc1 = [w.shape[1] // 2 for w in (w_qkv, w_proj, w_fc1)]
    line = Line()
    if fits:
        all_qkv = Gather(grid, line, [cast_qkv])
        all_qkv.first()
        place = line(place)
    labels = lax.all_to_all(
        jnp.broadcast_to(class_label, (grid.count,)), AXES, 0, 0, tiled=True
    )
    labels = jnp.take(labels, grid.sources(here))
    cast_ada = w_ada.astype(bf16)
    cast_table = w_table.astype(bf16)
    onehot = (labels[:, None] == jnp.arange(cast_table.shape[0])[None, :]).astype(bf16)
    cond = jnp.dot(onehot, cast_table, preferred_element_type=f32)
    silu_out, silu_back = jax.vjp(jax.nn.silu, cond)
    lifted_low = silu_out.astype(bf16)

    ada = jnp.dot(lifted_low, cast_ada, preferred_element_type=f32)
    flips = grid.bits()
    along = len(flips) - 2
    ada = Scatter(grid, line, ada.reshape(grid.count, -1, 128))
    if fits:
        ada.start()
        line.arrive([ada, all_qkv])
        ada.add()
        all_qkv.second()
        ada.start()
        line.arrive([ada])
        ada.add()
        line.arrive([all_qkv])
        all_qkv.third()
        all_rest = Gather(grid, line, [cast_proj, cast_fc1])
        all_rest.first()
        ada.start()
        line.arrive([ada])
        ada.add()
        line.arrive([all_qkv])
        all_qkv.fourth()
        ada.start()
        line.arrive([ada, all_rest])
        all_rest.second()
        ada.add()
        ada.start()
        bias = mask(line(length))
        bias, bias_t, all_qkv.near = line.arrive(
            [all_qkv, all_rest], bias, bias.T, all_qkv.near
        )
        pieces_qkv = all_qkv.pieces()
        all_rest.third()
        line.arrive([ada])
        ada.add()
    else:
        while ada.flips:
            ada.start()
            ada.add()
        bias = mask(length)
        bias_t = bias.T
    ada = ada.rows.reshape(1, 6 * width)
    gamma_one, scale_one, shift_one, gamma_two, scale_two, shift_two = [
        ada[:, i * width : (i + 1) * width] for i in range(6)
    ]

    def half_columns(rhs, core, groups=1):
        half = rhs.shape[1] // groups // 2
        parts = [
            lax.dynamic_slice_in_dim(rhs, (2 * i + core) * half, half, 1) for i in range(groups)
        ]
        return jnp.concatenate(parts, axis=1)

    def weight_grad(lhs, other_lhs, rhs, take, groups):
        half = take.shape[1]
        size = grid.size
        rows = lhs.shape[1] // grid.count
        mine = half_columns(rhs, here["c"], groups)
        both = jnp.concatenate([mine, take], axis=0)
        grad = contract_rows(jnp.concatenate([lhs, other_lhs], axis=0), both)
        grad = grad.reshape(size["z"], size["x"], 2, size["y"], rows, half)
        middle = half // 2
        one = grid.scatter_sum(grad[..., :middle], "y", 3, here)
        two = grid.scatter_sum(grad[..., middle:], "x", 1, here)
        one = grid.scatter_sum(one, "x", 1, here)
        two = grid.scatter_sum(two, "y", 2, here)
        both = grid.scatter_sum(jnp.concatenate([one, two], axis=-1), "z", 0, here)
        keep = lax.dynamic_index_in_dim(both, here["c"], 0, keepdims=False)
        give = lax.dynamic_index_in_dim(both, 1 - here["c"], 0, keepdims=False)
        take = grid.shift(give, "c", 1)
        low = jnp.where(here["c"] == 0, keep, take).reshape(rows, groups, 1, half // groups)
        high = jnp.where(here["c"] == 0, take, keep).reshape(rows, groups, 1, half // groups)
        return jnp.concatenate([low, high], axis=2).reshape(rows, 2 * half)

    tokens = block_in[0].astype(f32)
    hidden, modulate_one = jax.vjp(modulate, tokens, scale_one, shift_one)
    hidden_low = hidden.astype(bf16)
    if fits:
        hidden_low, pieces_qkv[4:] = line(hidden_low, pieces_qkv[4:])
        wide_qkv, packed = gather_dot(
            place, hidden_low, pieces_qkv, 0, half_qkv, [bf16], True, "gather_qkv"
        )
        packed = line.arrive([all_rest], packed)
        all_rest.fourth()
        all_fc2 = Gather(grid, line, [cast_fc2])
        all_fc2.first()
        packed = line(packed)
    else:
        wide_qkv = lax.all_gather(cast_qkv, AXES, axis=0, tiled=True)
        packed = jnp.dot(hidden_low, wide_qkv, preferred_element_type=f32).astype(bf16)
    pairs = width // 128
    heads = attend_forward(packed, bias, 0, pairs // 2)
    if fits:
        heads, all_rest.near = line.arrive([all_fc2], heads, all_rest.near)
        all_fc2.second()
    packed = line(packed)
    heads = attend_forward(packed, bias, pairs // 2, pairs, heads)
    if fits:
        heads = line.arrive([all_rest, all_fc2], *heads)
        pieces_rest = all_rest.pieces()
        all_fc2.third()
    context, lse = heads
    if fits:
        context, pieces_rest[4:] = line(context, pieces_rest[4:])
        wide_proj, attended = gather_dot(
            place, context, pieces_rest, 0, half_proj, [f32], True, "gather_proj"
        )
    else:
        wide_proj = lax.all_gather(cast_proj, AXES, axis=0, tiled=True)
        attended = jnp.dot(context, wide_proj, preferred_element_type=f32)
    if fits:
        attended = line.arrive([all_fc2], attended)
        all_fc2.fourth()
        attended = line(attended)
    middle = tokens + gamma_one * attended
    second, modulate_two = jax.vjp(modulate, middle, scale_two, shift_two)
    if not fits:
        upstream = cotangent[0].astype(f32) * valid
        d_branch = (upstream * gamma_two).astype(bf16)
        give = half_columns(d_branch, 1 - here["c"])
    second_low = line(second.astype(bf16))
    second_other = grid.shift(second_low, "c", 1)
    if fits:
        wide_fc1, slope, activated_low = gather_dot(
            place, second_low, pieces_rest, half_proj, half_fc1, [bf16, bf16], True, "gather_fc1"
        )
        activated_low, gradient = line(activated_low, cotangent[0])
        upstream = gradient.astype(f32) * valid
        d_branch = (upstream * gamma_two).astype(bf16)
        give = half_columns(d_branch, 1 - here["c"])
        slope, activated_low, second_other, d_branch, give = line.arrive(
            [all_fc2], slope, activated_low, second_other, d_branch, give
        )
        pieces_fc2 = all_fc2.pieces()
        pieces_fc2[4:] = line(pieces_fc2[4:])
    else:
        wide_fc1 = lax.all_gather(cast_fc1, AXES, axis=0, tiled=True)
        inner = jnp.dot(second_low, wide_fc1, preferred_element_type=f32)
        slope, activated = gelu_and_slope(inner)
        activated_low = activated.astype(bf16)
    activated_low, context, hidden_low = line(activated_low, context, hidden_low)
    activated_other = grid.shift(activated_low, "c", 1)
    context_other = grid.shift(context, "c", 1)
    hidden_other = grid.shift(hidden_low, "c", 1)
    take = grid.shift(give, "c", 1)
    if fits:
        rows_in, rows_out = w_qkv.shape[0], w_fc2.shape[0]
        d_branch = line(d_branch)
        d_inner_low, give, activated_other, take, context_other, hidden_other = line(
            *gelu_back_dot(place, d_branch, slope, pieces_fc2),
            activated_other,
            take,
            context_other,
            hidden_other,
        )
        pair_fc2 = (activated_low, activated_other, d_branch, take, 1)
        sum_two = GradSum(grid, line, here, place, [pair_fc2], rows_out, 256)
    else:
        wide_fc2 = lax.all_gather(cast_fc2, AXES, axis=0, tiled=True)
        sum_fc2 = weight_grad(activated_low, activated_other, d_branch, take, 1)
        d_inner_low = (contract_cols(d_branch, wide_fc2) * slope).astype(bf16)
        give = half_columns(d_inner_low, 1 - here["c"])
    take_inner = grid.shift(give, "c", 1)
    d_inner_low = line(d_inner_low)
    if fits:
        rows = [1.0 + scale_two, gamma_one, jnp.zeros((6, width), f32)]
        d_middle, d_attended, give, d_context, sums = line(
            *modulate_back(
                place,
                d_inner_low,
                wide_fc1,
                jnp.concatenate(rows, axis=0),
                middle,
                cotangent[0],
                attended,
                wide_proj,
            )
        )
        d_scale_two, d_shift_two, d_gamma_one = sums[0:1], sums[1:2], sums[2:3]
    else:
        d_second = contract_cols(d_inner_low, wide_fc1)
        d_middle_part, d_scale_two, d_shift_two = modulate_two(d_second)
        d_middle = upstream + d_middle_part
        d_gamma_one = jnp.sum(d_middle * attended, axis=0, keepdims=True)
        d_attended = (d_middle * gamma_one).astype(bf16)
        give = half_columns(d_attended, 1 - here["c"])
        d_context = contract_cols(d_attended, wide_proj).astype(bf16)
    take = grid.shift(give, "c", 1)
    if fits:
        take_inner = line.arrive([sum_two], take_inner)
        sum_two.second()
        take = line(take)
    pair_fc1 = (second_low, second_other, d_inner_low, take_inner, 1)
    pair_proj = (context, context_other, d_attended, take, 1)
    if fits:
        sum_mid = GradSum(
            grid, line, here, place, [pair_fc1, pair_proj], rows_in, 256, [sum_two]
        )
        sum_two.third()
    else:
        sum_fc1, sum_proj = weight_grad(*pair_fc1), weight_grad(*pair_proj)
    d_context = line(d_context)
    d_packed, give = attend_backward(place, packed, d_context, lse, bias_t)
    if fits:
        d_packed, give = line.arrive([sum_two, sum_mid], d_packed, give)
    take = grid.shift(give, "c", 1)
    if fits:
        sum_mid.second()
        sum_two.fourth()
        take = line(take)
        pair_qkv = (hidden_low, hidden_other, d_packed, take, 3)
        sum_last = GradSum(
            grid, line, here, place, [pair_qkv], rows_in, 256, [sum_two, sum_mid]
        )
        sum_mid.third()
        sum_two.fifth()
    else:
        sum_qkv = weight_grad(hidden_low, hidden_other, d_packed, take, 3)
    d_packed = line(d_packed)
    if fits:
        rows = [1.0 + scale_one, jnp.zeros((7, width), f32)]
        grad_in, sums = line(
            *modulate_back(
                place, d_packed, wide_qkv, jnp.concatenate(rows, axis=0), block_in[0], d_middle
            )
        )
        d_scale_one, d_shift_one = sums[0:1], sums[1:2]
    else:
        d_hidden = contract_cols(d_packed, wide_qkv)
        d_tokens, d_scale_one, d_shift_one = modulate_one(d_hidden)
        grad_in = d_middle + d_tokens
    if fits:
        line.arrive([sum_last, sum_mid])
        sum_last.second()
        sum_mid.fourth()
        activated_low = line(activated_low)
        (branch,) = gather_dot(
            place, activated_low, pieces_fc2, 0, width // 2, [f32], False, "gather_fc2"
        )
        branch = line.arrive([sum_last, sum_mid], branch)
        sum_last.third()
        sum_mid.fifth()
        branch = line(branch)
    else:
        branch = jnp.dot(activated_low, wide_fc2, preferred_element_type=f32)
    block_out = ((middle + gamma_two * branch) * valid).astype(bf16)
    d_gamma_two = jnp.sum(upstream * branch, axis=0, keepdims=True)
    d_ada = jnp.concatenate(
        [d_gamma_one, d_scale_one, d_shift_one, d_gamma_two, d_scale_two, d_shift_two], axis=0
    ).astype(bf16)
    every_ada = grid.gather_all(line(d_ada.reshape(-1, 128)), flips[:1])
    if fits:
        every_ada = line.arrive([sum_last], every_ada)
        sum_last.fourth()
        for done in (sum_two, sum_mid):
            done.take, done.keep = line(done.take, done.keep)
    every_ada = grid.gather_all(every_ada, flips[1:2])
    if fits:
        every_ada = line.arrive([sum_last], every_ada)
        sum_last.fifth()
    every_ada = grid.gather_all(every_ada, flips[2:])
    every_ada = every_ada.reshape(grid.count, 6 * width)
    sum_ada = contract_rows(lifted_low, every_ada)
    (d_cond,) = silu_back(contract_cols(every_ada, cast_ada))
    sum_table = lax.dot_general(
        onehot.astype(f32), d_cond, (((0,), (0,)), ((), ())), precision=highest
    )
    if fits:
        (sum_fc2,) = sum_two.result()
        sum_fc1, sum_proj = sum_mid.result()
        (sum_qkv,) = sum_last.result()
        sum_qkv = sum_qkv + line.last[0, 0]
    counter = f32(STEP)
    bias_one = 1.0 - jnp.power(f32(0.5), counter)
    bias_two = 1.0 - jnp.power(f32(0.5), counter)
    rates = learn_rates()
    updates = [
        adamw(w, g, m, v, bias_one, bias_two, rate)
        for w, g, m, v, rate in zip(
            (w_qkv, w_proj, w_fc1, w_fc2, w_ada, w_table),
            (sum_qkv, sum_proj, sum_fc1, sum_fc2, sum_ada, sum_table),
            (m_qkv, m_proj, m_fc1, m_fc2, m_ada, m_table),
            (v_qkv, v_proj, v_fc1, v_fc2, v_ada, v_table),
            rates,
        )
    ]
    return (block_out[None], grad_in[None]) + tuple(
        update[kind] for kind in range(4) for update in updates
    )


def solution(mesh):
    grid = Grid(mesh.shape["fsdp"], mesh.shape["grp"])
    items = P(AXES, None, None)
    vector = P(AXES)
    rows = P(AXES, None)
    columns = P(None, AXES)
    weights = (rows, rows, rows, rows, rows, columns)

    def run(*arrays):
        return per_device(grid, *arrays)

    return jax.shard_map(
        run,
        mesh=mesh,
        in_specs=(items, items, vector, vector) + weights * 3,
        out_specs=(items, items) + weights * 4,
        check_vma=False,
    )
```

profile of v0, /device:TPU:0, one launch (start us, length us, event | category | flops | bytes accessed | tf_op | source)
XLA Modules:
  0.0 418.5 jit_solution(16307870223465709122)
XLA Ops:
  2.0 7.3 %all-to-all-start = ((s32[32,1,1]{2,1,0:T(1,128)}), s32[32,1,1]{2,1,0:T(1,128)S(1)}, u32[]{:S(2)}, u32[]{:S(2)}) async-start(s32[32,1,1]{2,1,0:T(1,128)} %broadcast_in_dim.121), calls=%async_computation | async-start | bytes 32768 | tf_op jit(solution)/shard_map/all_to_all | solution.py:1090
  10.4 2.7 collective-permute-start.1
  23.1 1.5 collective-permute-start.2
  24.6 1.5 collective-permute-start.3
  26.2 3.9 collective-permute-done.2
  30.1 5.4 %collective-permute-done.3 = bf16[2,32,3072]{2,1,0:T(8,128)(2,1)S(1)} collective-permute-done((bf16[2,32,3072]{2,1,0:T(8,128)(2,1)S(1)}, bf16[2,32,3072]{2,1,0:T(8,128)(2,1)S(1)}, u32[]{:S(2)}, u32[]{:S(2)}) %collective-permute-start.3) | collective-permute-done | bytes 393248 | tf_op jit(solution)/shard_map/ppermute | solution.py:1029
  35.6 1.6 collective-permute-start.4
  38.8 1.8 collective-permute-start.8
  41.4 7.1 %collective-permute-done.5 = bf16[4,32,1536]{2,1,0:T(8,128)(2,1)S(1)} collective-permute-done((bf16[4,32,1536]{2,1,0:T(8,128)(2,1)S(1)}, bf16[4,32,1536]{2,1,0:T(8,128)(2,1)S(1)}, u32[]{:S(2)}, u32[]{:S(2)}) %collective-permute-start.5) | collective-permute-done | bytes 393248 | tf_op jit(solution)/shard_map/ppermute | solution.py:1023
  48.7 2.1 collective-permute-start.7
  52.1 4.0 collective-permute-done.8
  56.1 1.5 collective-permute-start.9
  58.4 2.1 and_select_fusion
  60.5 12.7 %collective-permute-done.11 = bf16[2,32,5120]{2,1,0:T(8,128)(2,1)S(1)} collective-permute-done((bf16[2,32,5120]{2,1,0:T(8,128)(2,1)S(1)}, bf16[2,32,5120]{2,1,0:T(8,128)(2,1)S(1)}, u32[]{:S(2)}, u32[]{:S(2)}) %collective-permute-start.11) | collective-permute-done | bytes 655392 | tf_op jit(solution)/shard_map/ppermute | solution.py:1029
  75.3 1.7 collective-permute-done.14
  77.0 1.5 collective-permute-start.17
  78.5 1.3 collective-permute-start.18
  79.8 1.7 fusion.5.x_ref.refs_0_
  82.4 11.2 %gather_qkv.1 = (bf16[1024,3072]{1,0:T(8,128)(2,1)}, bf16[680,3072]{1,0:T(8,128)(2,1)}) custom-call(s32[5]{0:T(128)} %stack.50.place_ref, bf16[680,1024]{1,0:T(8,128)(2,1)} %fusion.5.x_ref.refs_0_, bf16[2,4,32,1536]{3,2,1,0:T(8,128)(2,1)} %copy-done.41, bf16[2,4,32,1536]{3,2,1,0:T(8,128)(2,1)} %copy-done.40, bf16[2,4,32,1536]{3,2,1,0:T(8,128)(2,1)} %copy-done.51, ...), custom_call_target="tpu_custom_call" | custom-call | flops 100270080 | bytes 228864 | tf_op jit(solution)/shard_map/gather_qkv/pallas_call | solution.py:346
  93.6 1.5 pad_maximum_fusion.1.refs_1_
  95.2 2.0 pad_maximum_fusion.refs_0_
  99.0 3.3 collective-permute-start.19
  102.3 11.0 %attend.2 = (bf16[680,1024]{1,0:T(8,128)(2,1)S(1)}, f32[8,2,680]{2,1,0:T(2,128)S(1)}) custom-call(bf16[680,3072]{1,0:T(8,128)(2,1)S(1)} %copy-done, bf16[680,3072]{1,0:T(8,128)(2,1)S(1)} %copy-done, bf16[680,3072]{1,0:T(8,128)(2,1)S(1)} %copy-done, f32[680,680]{1,0:T(8,128)S(1)} %get-tuple-element.416.bias_ref), custom_call_target="tpu_custom_call" | custom-call | flops 36992000 | bytes 65280 | tf_op jit(solution)/shard_map/attend/pallas_call | solution.py:129
  114.7 23.6 %attend.3 = (bf16[680,1024]{1,0:T(8,128)(2,1)S(1)}, f32[8,2,680]{2,1,0:T(2,128)S(1)}) custom-call(bf16[680,3072]{1,0:T(8,128)(2,1)S(1)} %copy-done, bf16[680,3072]{1,0:T(8,128)(2,1)S(1)} %copy-done, bf16[680,3072]{1,0:T(8,128)(2,1)S(1)} %copy-done, f32[680,680]{1,0:T(8,128)S(1)} %get-tuple-element.416.bias_ref, ...), custom_call_target="tpu_custom_call", output_to_operand_aliasing={{0}: (4, {}), {1}: (5, {})} | custom-call | flops 36992000 | bytes 65280 | tf_op jit(solution)/shard_map/attend/pallas_call | solution.py:129
  140.2 1.6 collective-permute-start.27
  145.5 6.8 %gather_proj.1 = (bf16[1024,1024]{1,0:T(8,128)(2,1)}, f32[680,1024]{1,0:T(8,128)}) custom-call(s32[5]{0:T(128)} %stack.50.place_ref, bf16[680,1024]{1,0:T(8,128)(2,1)} %copy-done.4, bf16[2,4,32,2560]{3,2,1,0:T(8,128)(2,1)} %copy-done.30, bf16[2,4,32,2560]{3,2,1,0:T(8,128)(2,1)} %copy-done.29, bf16[2,4,32,2560]{3,2,1,0:T(8,128)(2,1)} %copy-done.34, ...), custom_call_target="tpu_custom_call" | custom-call | flops 33423360 | bytes 76288 | tf_op jit(solution)/shard_map/gather_proj/pallas_call | solution.py:346
  152.2 1.9 collective-permute-done.27
  158.5 1.6 add_convert_fusion.x_ref.refs_0_
  163.2 16.9 %gather_fc1.1 = (bf16[1024,4096]{1,0:T(8,128)(2,1)}, bf16[680,4096]{1,0:T(8,128)(2,1)}, bf16[680,4096]{1,0:T(8,128)(2,1)}) custom-call(s32[5]{0:T(128)} %stack.50.place_ref, bf16[680,1024]{1,0:T(8,128)(2,1)} %add_convert_fusion.x_ref.refs_0_, bf16[2,4,32,2560]{3,2,1,0:T(8,128)(2,1)} %copy-done.30, bf16[2,4,32,2560]{3,2,1,0:T(8,128)(2,1)} %copy-done.29, ...), custom_call_target="tpu_custom_call" | custom-call | flops 133693440 | bytes 305152 | tf_op jit(solution)/shard_map/gather_fc1/pallas_call | solution.py:346
  181.4 4.5 %collective-permute-done.29.refs_2_ = bf16[2,4,128,512]{3,2,1,0:T(8,128)(2,1)} collective-permute-done((bf16[2,4,128,512]{3,2,1,0:T(8,128)(2,1)}, bf16[2,4,128,512]{3,2,1,0:T(8,128)(2,1)}, u32[]{:S(2)}, u32[]{:S(2)}) %collective-permute-start.29) | collective-permute-done | bytes 1048608 | tf_op jit(solution)/shard_map/ppermute | solution.py:1029
  187.5 2.4 collective-permute-done.34.refs_6_
  189.9 1.5 collective-permute-done.35.refs_7_
  192.5 13.1 %gelu_back.1 = (bf16[680,4096]{1,0:T(8,128)(2,1)}, bf16[680,2048]{1,0:T(8,128)(2,1)}) custom-call(s32[5]{0:T(128)} %stack.50.place_ref, bf16[680,1024]{1,0:T(8,128)(2,1)} %copy-done.27, bf16[680,4096]{1,0:T(8,128)(2,1)} %get-tuple-element.473.slope_ref, bf16[2,4,128,512]{3,2,1,0:T(8,128)(2,1)} %pad_maximum_fusion.2.refs_0_, ...), custom_call_target="tpu_custom_call" | custom-call | flops 133693440 | bytes 610304 | tf_op jit(solution)/shard_map/gelu_back/pallas_call | solution.py:580
  206.3 11.9 %weight_grad_rows.1 = (bf16[2,4,2,128,256]{4,3,2,1,0:T(8,128)(2,1)}, bf16[2,4,2,128,256]{4,3,2,1,0:T(8,128)(2,1)}, bf16[2,4,2,128,256]{4,3,2,1,0:T(8,128)(2,1)}, bf16[2,4,2,128,256]{4,3,2,1,0:T(8,128)(2,1)}) custom-call(s32[5]{0:T(128)} %stack.50.place_ref, bf16[680,4096]{1,0:T(8,128)(2,1)} %get-tuple-element.616.own_ref.x_ref, ...), custom_call_target="tpu_custom_call" | custom-call | flops 89128960 | bytes 261376 | tf_op jit(solution)/shard_map/weight_grad_rows/pallas_call | solution.py:731
  219.6 19.9 %modulate_back.2 = (f32[680,1024]{1,0:T(8,128)}, bf16[680,1024]{1,0:T(8,128)(2,1)S(1)}, bf16[680,512]{1,0:T(8,128)(2,1)S(1)}, bf16[680,1024]{1,0:T(8,128)(2,1)S(1)}, f32[8,1024]{1,0:T(8,128)S(1)}) custom-call(s32[5]{0:T(128)S(1)} %copy-done.21, bf16[680,4096]{1,0:T(8,128)(2,1)} %get-tuple-element.494.x_ref.refs_2_, ...), custom_call_target="tpu_custom_call" | custom-call | flops 167116800 | bytes 392192 | tf_op jit(solution)/shard_map/modulate_back/pallas_call | solution.py:489
  239.6 4.0 collective-permute-done.40.refs_1_.refs_3_
  243.9 2.6 add_second.3
  247.3 1.5 collective-permute-start.45
  248.8 17.9 %weight_grad.2 = (bf16[2,4,2,32,1280]{4,3,2,1,0:T(8,128)(2,1)}, bf16[2,4,2,32,1280]{4,3,2,1,0:T(8,128)(2,1)}, bf16[2,4,2,32,1280]{4,3,2,1,0:T(8,128)(2,1)}, bf16[2,4,2,32,1280]{4,3,2,1,0:T(8,128)(2,1)}) custom-call(s32[5]{0:T(128)} %stack.50.place_ref, bf16[680,1024]{1,0:T(8,128)(2,1)} %add_convert_fusion.x_ref.refs_0_, ...), custom_call_target="tpu_custom_call" | custom-call | flops 167116800 | bytes 332160 | tf_op jit(solution)/shard_map/weight_grad/pallas_call | solution.py:685
  268.6 2.0 add_third.3
  271.5 1.6 copy-done.8
  273.1 1.3 copy-done.20
  274.4 31.8 %attend_back.1 = (bf16[680,3072]{1,0:T(8,128)(2,1)S(1)}, bf16[680,1536]{1,0:T(8,128)(2,1)S(1)}) custom-call(s32[5]{0:T(128)S(1)} %copy-done.22, bf16[680,3072]{1,0:T(8,128)(2,1)S(1)} %copy-done.1, bf16[680,3072]{1,0:T(8,128)(2,1)S(1)} %copy-done.1, bf16[680,3072]{1,0:T(8,128)(2,1)S(1)} %copy-done.1, bf16[680,1024]{1,0:T(8,128)(2,1)S(1)} %copy-done.20, ...), custom_call_target="tpu_custom_call" | custom-call | flops 147968000 | bytes 174080 | tf_op jit(solution)/shard_map/attend_back/pallas_call | solution.py:236
  306.4 2.9 add_second.4
  311.3 1.5 collective-permute-start.52
  312.8 1.3 add_fourth.3
  314.1 1.9 collective-permute-start.50
  316.1 11.0 %weight_grad.3 = (bf16[2,4,2,32,768]{4,3,2,1,0:T(8,128)(2,1)}, bf16[2,4,2,32,768]{4,3,2,1,0:T(8,128)(2,1)}, bf16[2,4,2,32,768]{4,3,2,1,0:T(8,128)(2,1)}, bf16[2,4,2,32,768]{4,3,2,1,0:T(8,128)(2,1)}) custom-call(s32[5]{0:T(128)} %stack.50.place_ref, bf16[680,1024]{1,0:T(8,128)(2,1)} %fusion.5.x_ref.refs_0_, ...), custom_call_target="tpu_custom_call" | custom-call | flops 100270080 | bytes 190592 | tf_op jit(solution)/shard_map/weight_grad/pallas_call | solution.py:685
  327.1 1.3 collective-permute-done.50.refs_1_.refs_3_
  331.3 2.1 add_third.4
  336.0 16.9 %modulate_back.3 = (f32[680,1024]{1,0:T(8,128)}, f32[8,1024]{1,0:T(8,128)S(1)}) custom-call(s32[5]{0:T(128)S(1)} %copy-done.23, bf16[680,3072]{1,0:T(8,128)(2,1)} %copy-done.3, bf16[1024,3072]{1,0:T(8,128)(2,1)} %get-tuple-element.589.w_ref, f32[8,1024]{1,0:T(8,128)S(1)} %concatenate.96.rows_ref, bf16[680,1024]{1,0:T(8,128)(2,1)S(1)} %bitcast.114, ...), custom_call_target="tpu_custom_call" | custom-call | flops 100270080 | bytes 337664 | tf_op jit(solution)/shard_map/modulate_back/pallas_call | solution.py:489
  356.8 2.7 collective-permute-start.58
  359.6 12.9 %gather_fc2.1 = f32[680,1024]{1,0:T(8,128)} custom-call(s32[5]{0:T(128)} %stack.50.place_ref, bf16[680,4096]{1,0:T(8,128)(2,1)} %get-tuple-element.616.own_ref.x_ref, bf16[2,4,128,512]{3,2,1,0:T(8,128)(2,1)} %pad_maximum_fusion.2.refs_0_, bf16[2,4,128,512]{3,2,1,0:T(8,128)(2,1)} %pad_maximum_fusion.3.refs_1_, ...), custom_call_target="tpu_custom_call" | custom-call | flops 133693440 | bytes 174592 | tf_op jit(solution)/shard_map/gather_fc2/pallas_call | solution.py:346
  375.2 3.6 multiply_reduce_fusion
  380.2 6.0 %collective-permute-done.59.refs_1_.refs_3_ = bf16[2,2,32,1536]{3,2,1,0:T(8,128)(2,1)S(1)} collective-permute-done((bf16[2,2,32,1536]{3,2,1,0:T(8,128)(2,1)S(1)}, bf16[2,2,32,1536]{3,2,1,0:T(8,128)(2,1)S(1)}, u32[]{:S(2)}, u32[]{:S(2)}) %collective-permute-start.59) | collective-permute-done | bytes 393248 | tf_op jit(solution)/shard_map/ppermute | solution.py:1029
  390.4 2.7 fusion.46
  393.2 1.5 fusion.48
  394.7 4.3 %collective-permute-done.63.refs_1_.refs_3_ = bf16[2,32,1536]{2,1,0:T(8,128)(2,1)S(1)} collective-permute-done((bf16[2,32,1536]{2,1,0:T(8,128)(2,1)S(1)}, bf16[2,32,1536]{2,1,0:T(8,128)(2,1)S(1)}, u32[]{:S(2)}, u32[]{:S(2)}) %collective-permute-start.63) | collective-permute-done | bytes 196640 | tf_op jit(solution)/shard_map/ppermute | solution.py:1029
  399.0 1.6 collective-permute-start.66
  401.3 1.8 collective-permute-done.66
  404.6 4.1 collective-permute-done.67
  409.0 2.1 fusion.52
  411.1 3.4 collective-permute-done.68
  414.9 2.3 fusion.44
  (344 shorter events, 68.1 us)
Async XLA Ops:
  2.0 17.0 %all-to-all-start = ((s32[32,1,1]{2,1,0:T(1,128)}), s32[32,1,1]{2,1,0:T(1,128)S(1)}, u32[]{:S(2)}, u32[]{:S(2)}) async-start(s32[32,1,1]{2,1,0:T(1,128)} %broadcast_in_dim.121), calls=%async_computation | async-start | bytes 32768 | tf_op jit(solution)/shard_map/all_to_all | solution.py:1090
  10.4 12.3 %collective-permute-start.1 = (bf16[32,3072]{1,0:T(8,128)(2,1)S(1)}, bf16[32,3072]{1,0:T(8,128)(2,1)S(1)}, u32[]{:S(2)}, u32[]{:S(2)}) collective-permute-start(bf16[32,3072]{1,0:T(8,128)(2,1)S(1)} %convert_element_type.75), channel_id=1, source_target_pairs={{0,16},{2,18},{4,20},{6,22},{8,24},{10,26},{12,28},{14,30},{16,0},... | collective-permute-start | bytes 589832 | tf_op jit(solution)/shard_map/ppermute | solution.py:1029
  23.1 7.0 %collective-permute-start.2 = (f32[2,2,2,48,128]{4,3,0,1,2:T(8,128)S(1)}, f32[2,2,2,48,128]{4,3,0,1,2:T(8,128)S(1)}, u32[]{:S(2)}, u32[]{:S(2)}) collective-permute-start(f32[2,2,2,48,128]{4,3,0,1,2:T(8,128)S(1)} %slice_bitcast_fusion), channel_id=1, source_target_pairs={{0,4},{2,6},{4,0},{6,2},{8,12},{10,14},{12,8},{14,10},{16,20},{18,... | collective-permute-start | bytes 589832 | tf_op jit(solution)/shard_map/ppermute | solution.py:1029
  24.6 10.9 %collective-permute-start.3 = (bf16[2,32,3072]{2,1,0:T(8,128)(2,1)S(1)}, bf16[2,32,3072]{2,1,0:T(8,128)(2,1)S(1)}, u32[]{:S(2)}, u32[]{:S(2)}) collective-permute-start(bf16[2,32,3072]{2,1,0:T(8,128)(2,1)S(1)} %pad_maximum_fusion.14), channel_id=1, source_target_pairs={{0,8},{2,10},{4,12},{6,14},{8,0},{10,2},{12,4},{14,6},{16,24},{18,... | collective-permute-start | bytes 1179656 | tf_op jit(solution)/shard_map/ppermute | solution.py:1029
  35.6 5.7 %collective-permute-start.4 = (f32[2,2,48,128]{3,2,0,1:T(8,128)S(1)}, f32[2,2,48,128]{3,2,0,1:T(8,128)S(1)}, u32[]{:S(2)}, u32[]{:S(2)}) collective-permute-start(f32[2,2,48,128]{3,2,0,1:T(8,128)S(1)} %slice_bitcast_fusion.2), channel_id=1, source_target_pairs={{0,1},{1,0},{2,3},{3,2},{4,5},{5,4},{6,7},{7,6},{8,9},{9,8},{10,11... | collective-permute-start | bytes 294920 | tf_op jit(solution)/shard_map/ppermute | solution.py:1023
  37.7 10.8 %collective-permute-start.5 = (bf16[4,32,1536]{2,1,0:T(8,128)(2,1)S(1)}, bf16[4,32,1536]{2,1,0:T(8,128)(2,1)S(1)}, u32[]{:S(2)}, u32[]{:S(2)}) collective-permute-start(bf16[4,32,1536]{2,1,0:T(8,128)(2,1)S(1)} %get-tuple-element.368), channel_id=1, source_target_pairs={{0,1},{1,0},{2,3},{3,2},{4,5},{5,4},{6,7},{7,6},{8,9},{9,8},{10,11... | collective-permute-start | bytes 1179656 | tf_op jit(solution)/shard_map/ppermute | solution.py:1023
  38.3 10.2 %collective-permute-start.6 = (bf16[4,32,1536]{2,1,0:T(8,128)(2,1)S(1)}, bf16[4,32,1536]{2,1,0:T(8,128)(2,1)S(1)}, u32[]{:S(2)}, u32[]{:S(2)}) collective-permute-start(bf16[4,32,1536]{2,1,0:T(8,128)(2,1)S(1)} %get-tuple-element.369), channel_id=1, source_target_pairs={{0,4},{2,6},{4,0},{6,2},{8,12},{10,14},{12,8},{14,10},{16,20},{18,... | collective-permute-start | bytes 1179656 | tf_op jit(solution)/shard_map/ppermute | solution.py:1029
  38.8 17.3 %collective-permute-start.8 = (bf16[32,5120]{1,0:T(8,128)(2,1)S(1)}, bf16[32,5120]{1,0:T(8,128)(2,1)S(1)}, u32[]{:S(2)}, u32[]{:S(2)}) collective-permute-start(bf16[32,5120]{1,0:T(8,128)(2,1)S(1)} %pad_maximum_fusion.18), channel_id=1, source_target_pairs={{0,16},{2,18},{4,20},{6,22},{8,24},{10,26},{12,28},{14,30},{16,0},... | collective-permute-start | bytes 983048 | tf_op jit(solution)/shard_map/ppermute | solution.py:1029
  48.7 8.9 %collective-permute-start.7 = (f32[2,48,128]{2,1,0:T(8,128)S(1)}, f32[2,48,128]{2,1,0:T(8,128)S(1)}, u32[]{:S(2)}, u32[]{:S(2)}) collective-permute-start(f32[2,48,128]{2,1,0:T(8,128)S(1)} %slice_bitcast_fusion.4), channel_id=1, source_target_pairs={{0,16},{2,18},{4,20},{6,22},{8,24},{10,26},{12,28},{14,30},{16,0},... | collective-permute-start | bytes 147464 | tf_op jit(solution)/shard_map/ppermute | solution.py:1029
  50.8 23.5 %collective-permute-start.10 = (bf16[2,4,32,1536]{3,2,1,0:T(8,128)(2,1)S(1)}, bf16[2,4,32,1536]{3,2,1,0:T(8,128)(2,1)S(1)}, u32[]{:S(2)}, u32[]{:S(2)}) collective-permute-start(bf16[2,4,32,1536]{3,2,1,0:T(8,128)(2,1)S(1)} %pad_maximum_fusion.5.refs_1_), channel_id=1, source_target_pairs={{0,1},{1,0},{2,3},{3,2},{4,5},{5,4},{6,7},{7,6},{8,9},{9,8},{10,11... | collective-permute-start | bytes 2359304 | tf_op jit(solution)/shard_map/ppermute | solution.py:1023
  51.6 22.7 %collective-permute-start.13 = (bf16[2,4,32,1536]{3,2,1,0:T(8,128)(2,1)S(1)}, bf16[2,4,32,1536]{3,2,1,0:T(8,128)(2,1)S(1)}, u32[]{:S(2)}, u32[]{:S(2)}) collective-permute-start(bf16[2,4,32,1536]{3,2,1,0:T(8,128)(2,1)S(1)} %pad_maximum_fusion.5.refs_1_), channel_id=1, source_target_pairs={{0,2},{2,0},{4,6},{6,4},{8,10},{10,8},{12,14},{14,12},{16,18},{18,... | collective-permute-start | bytes 2359304 | tf_op jit(solution)/shard_map/ppermute | solution.py:1029
  51.6 22.7 %collective-permute-start.12 = (bf16[2,4,32,1536]{3,2,1,0:T(8,128)(2,1)S(1)}, bf16[2,4,32,1536]{3,2,1,0:T(8,128)(2,1)S(1)}, u32[]{:S(2)}, u32[]{:S(2)}) collective-permute-start(bf16[2,4,32,1536]{3,2,1,0:T(8,128)(2,1)S(1)} %pad_maximum_fusion.4.refs_0_), channel_id=1, source_target_pairs={{0,2},{2,0},{4,6},{6,4},{8,10},{10,8},{12,14},{14,12},{16,18},{18,... | collective-permute-start | bytes 2359304 | tf_op jit(solution)/shard_map/ppermute | solution.py:1029
  56.1 18.2 %collective-permute-start.9 = (bf16[2,4,32,1536]{3,2,1,0:T(8,128)(2,1)S(1)}, bf16[2,4,32,1536]{3,2,1,0:T(8,128)(2,1)S(1)}, u32[]{:S(2)}, u32[]{:S(2)}) collective-permute-start(bf16[2,4,32,1536]{3,2,1,0:T(8,128)(2,1)S(1)} %pad_maximum_fusion.4.refs_0_), channel_id=1, source_target_pairs={{0,4},{2,6},{4,0},{6,2},{8,12},{10,14},{12,8},{14,10},{16,20},{18,... | collective-permute-start | bytes 2359304 | tf_op jit(solution)/shard_map/ppermute | solution.py:1029
  58.3 14.9 %collective-permute-start.11 = (bf16[2,32,5120]{2,1,0:T(8,128)(2,1)S(1)}, bf16[2,32,5120]{2,1,0:T(8,128)(2,1)S(1)}, u32[]{:S(2)}, u32[]{:S(2)}) collective-permute-start(bf16[2,32,5120]{2,1,0:T(8,128)(2,1)S(1)} %pad_maximum_fusion.6), channel_id=1, source_target_pairs={{0,8},{2,10},{4,12},{6,14},{8,0},{10,2},{12,4},{14,6},{16,24},{18,... | collective-permute-start | bytes 1966088 | tf_op jit(solution)/shard_map/ppermute | solution.py:1029
  74.4 7.1 %collective-permute-start.15 = (bf16[2,4,32,1536]{3,2,1,0:T(8,128)(2,1)S(1)}, bf16[2,4,32,1536]{3,2,1,0:T(8,128)(2,1)S(1)}, u32[]{:S(2)}, u32[]{:S(2)}) collective-permute-start(bf16[2,4,32,1536]{3,2,1,0:T(8,128)(2,1)S(1)} %collective-permute-done.9.refs_2_), channel_id=1, source_target_pairs={{0,2},{2,0},{4,6},{6,4},{8,10},{10,8},{12,14},{14,12},{16,18},{18,... | collective-permute-start | bytes 2359304 | tf_op jit(solution)/shard_map/ppermute | solution.py:1029
  74.5 8.0 %collective-permute-start.16 = (bf16[2,4,32,1536]{3,2,1,0:T(8,128)(2,1)S(1)}, bf16[2,4,32,1536]{3,2,1,0:T(8,128)(2,1)}, u32[]{:S(2)}, u32[]{:S(2)}) collective-permute-start(bf16[2,4,32,1536]{3,2,1,0:T(8,128)(2,1)S(1)} %collective-permute-done.10.refs_3_), channel_id=1, source_target_pairs={{0,2},{2,0},{4,6},{6,4},{8,10},{10,8},{12,14},{14,12},{16,18},{18,... | collective-permute-start | bytes 2359304 | tf_op jit(solution)/shard_map/ppermute | solution.py:1029
  77.0 16.6 %collective-permute-start.17 = (bf16[4,32,2560]{2,1,0:T(8,128)(2,1)S(1)}, bf16[4,32,2560]{2,1,0:T(8,128)(2,1)S(1)}, u32[]{:S(2)}, u32[]{:S(2)}) collective-permute-start(bf16[4,32,2560]{2,1,0:T(8,128)(2,1)S(1)} %pad_maximum_fusion.7), channel_id=1, source_target_pairs={{0,1},{1,0},{2,3},{3,2},{4,5},{5,4},{6,7},{7,6},{8,9},{9,8},{10,11... | collective-permute-start | bytes 1966088 | tf_op jit(solution)/shard_map/ppermute | solution.py:1023
  78.5 15.1 %collective-permute-start.18 = (bf16[4,32,2560]{2,1,0:T(8,128)(2,1)S(1)}, bf16[4,32,2560]{2,1,0:T(8,128)(2,1)}, u32[]{:S(2)}, u32[]{:S(2)}) collective-permute-start(bf16[4,32,2560]{2,1,0:T(8,128)(2,1)S(1)} %pad_maximum_fusion.8), channel_id=1, source_target_pairs={{0,4},{2,6},{4,0},{6,2},{8,12},{10,14},{12,8},{14,10},{16,20},{18,... | collective-permute-start | bytes 1966088 | tf_op jit(solution)/shard_map/ppermute | solution.py:1029
  97.1 16.7 %collective-permute-start.20 = (bf16[2,4,32,2560]{3,2,1,0:T(8,128)(2,1)S(1)}, bf16[2,4,32,2560]{3,2,1,0:T(8,128)(2,1)S(1)}, u32[]{:S(2)}, u32[]{:S(2)}) collective-permute-start(bf16[2,4,32,2560]{3,2,1,0:T(8,128)(2,1)S(1)} %pad_maximum_fusion.refs_0_), channel_id=1, source_target_pairs={{0,2},{2,0},{4,6},{6,4},{8,10},{10,8},{12,14},{14,12},{16,18},{18,... | collective-permute-start | bytes 3932168 | tf_op jit(solution)/shard_map/ppermute | solution.py:1029
  97.2 16.7 %collective-permute-start.21 = (bf16[2,4,32,2560]{3,2,1,0:T(8,128)(2,1)S(1)}, bf16[2,4,32,2560]{3,2,1,0:T(8,128)(2,1)S(1)}, u32[]{:S(2)}, u32[]{:S(2)}) collective-permute-start(bf16[2,4,32,2560]{3,2,1,0:T(8,128)(2,1)S(1)} %pad_maximum_fusion.1.refs_1_), channel_id=1, source_target_pairs={{0,2},{2,0},{4,6},{6,4},{8,10},{10,8},{12,14},{14,12},{16,18},{18,... | collective-permute-start | bytes 3932168 | tf_op jit(solution)/shard_map/ppermute | solution.py:1029
  97.7 40.7 %collective-permute-start.22 = (bf16[2,4,32,2560]{3,2,1,0:T(8,128)(2,1)S(1)}, bf16[2,4,32,2560]{3,2,1,0:T(8,128)(2,1)S(1)}, u32[]{:S(2)}, u32[]{:S(2)}) collective-permute-start(bf16[2,4,32,2560]{3,2,1,0:T(8,128)(2,1)S(1)} %pad_maximum_fusion.refs_0_), channel_id=1, source_target_pairs={{0,4},{2,6},{4,0},{6,2},{8,12},{10,14},{12,8},{14,10},{16,20},{18,... | collective-permute-start | bytes 3932168 | tf_op jit(solution)/shard_map/ppermute | solution.py:1029
  98.4 40.0 %collective-permute-start.23 = (bf16[2,4,32,2560]{3,2,1,0:T(8,128)(2,1)S(1)}, bf16[2,4,32,2560]{3,2,1,0:T(8,128)(2,1)S(1)}, u32[]{:S(2)}, u32[]{:S(2)}) collective-permute-start(bf16[2,4,32,2560]{3,2,1,0:T(8,128)(2,1)S(1)} %pad_maximum_fusion.1.refs_1_), channel_id=1, source_target_pairs={{0,1},{1,0},{2,3},{3,2},{4,5},{5,4},{6,7},{7,6},{8,9},{9,8},{10,11... | collective-permute-start | bytes 3932168 | tf_op jit(solution)/shard_map/ppermute | solution.py:1023
  99.0 14.9 %collective-permute-start.19 = (bf16[128,1024]{1,0:T(8,128)(2,1)S(1)}, bf16[128,1024]{1,0:T(8,128)(2,1)S(1)}, u32[]{:S(2)}, u32[]{:S(2)}) collective-permute-start(bf16[128,1024]{1,0:T(8,128)(2,1)S(1)} %convert_element_type.79), channel_id=1, source_target_pairs={{0,16},{2,18},{4,20},{6,22},{8,24},{10,26},{12,28},{14,30},{16,0},... | collective-permute-start | bytes 786440 | tf_op jit(solution)/shard_map/ppermute | solution.py:1029
  114.0 24.5 %collective-permute-start.24 = (bf16[2,128,1024]{2,1,0:T(8,128)(2,1)S(1)}, bf16[2,128,1024]{2,1,0:T(8,128)(2,1)S(1)}, u32[]{:S(2)}, u32[]{:S(2)}) collective-permute-start(bf16[2,128,1024]{2,1,0:T(8,128)(2,1)S(1)} %pad_maximum_fusion.9), channel_id=1, source_target_pairs={{0,8},{2,10},{4,12},{6,14},{8,0},{10,2},{12,4},{14,6},{16,24},{18,... | collective-permute-start | bytes 1572872 | tf_op jit(solution)/shard_map/ppermute | solution.py:1029
  139.5 4.9 %collective-permute-start.26 = (bf16[2,4,32,2560]{3,2,1,0:T(8,128)(2,1)S(1)}, bf16[2,4,32,2560]{3,2,1,0:T(8,128)(2,1)S(1)}, u32[]{:S(2)}, u32[]{:S(2)}) collective-permute-start(bf16[2,4,32,2560]{3,2,1,0:T(8,128)(2,1)S(1)} %collective-permute-done.23.refs_3_), channel_id=1, source_target_pairs={{0,2},{2,0},{4,6},{6,4},{8,10},{10,8},{12,14},{14,12},{16,18},{18,... | collective-permute-start | bytes 3932168 | tf_op jit(solution)/shard_map/ppermute | solution.py:1029
  140.2 13.9 %collective-permute-start.27 = (bf16[4,128,512]{2,1,0:T(8,128)(2,1)S(1)}, bf16[4,128,512]{2,1,0:T(8,128)(2,1)S(1)}, u32[]{:S(2)}, u32[]{:S(2)}) collective-permute-start(bf16[4,128,512]{2,1,0:T(8,128)(2,1)S(1)} %pad_maximum_fusion.10), channel_id=1, source_target_pairs={{0,1},{1,0},{2,3},{3,2},{4,5},{5,4},{6,7},{7,6},{8,9},{9,8},{10,11... | collective-permute-start | bytes 1572872 | tf_op jit(solution)/shard_map/ppermute | solution.py:1023
  141.8 13.6 %collective-permute-start.28 = (bf16[4,128,512]{2,1,0:T(8,128)(2,1)S(1)}, bf16[4,128,512]{2,1,0:T(8,128)(2,1)S(1)}, u32[]{:S(2)}, u32[]{:S(2)}) collective-permute-start(bf16[4,128,512]{2,1,0:T(8,128)(2,1)S(1)} %pad_maximum_fusion.11), channel_id=1, source_target_pairs={{0,4},{2,6},{4,0},{6,2},{8,12},{10,14},{12,8},{14,10},{16,20},{18,... | collective-permute-start | bytes 1572872 | tf_op jit(solution)/shard_map/ppermute | solution.py:1029
  160.1 26.9 %collective-permute-start.31 = (bf16[680,1024]{1,0:T(8,128)(2,1)}, bf16[680,1024]{1,0:T(8,128)(2,1)}, u32[]{:S(2)}, u32[]{:S(2)}) collective-permute-start(bf16[680,1024]{1,0:T(8,128)(2,1)} %add_convert_fusion.x_ref.refs_0_), channel_id=1, source_target_pairs={{0,2},{2,0},{4,6},{6,4},{8,10},{10,8},{12,14},{14,12},{16,18},{18,... | collective-permute-start | bytes 4177928 | tf_op jit(solution)/shard_map/ppermute | solution.py:988
  160.1 25.9 %collective-permute-start.29 = (bf16[2,4,128,512]{3,2,1,0:T(8,128)(2,1)}, bf16[2,4,128,512]{3,2,1,0:T(8,128)(2,1)}, u32[]{:S(2)}, u32[]{:S(2)}) collective-permute-start(bf16[2,4,128,512]{3,2,1,0:T(8,128)(2,1)} %pad_maximum_fusion.2.refs_0_), channel_id=1, source_target_pairs={{0,4},{2,6},{4,0},{6,2},{8,12},{10,14},{12,8},{14,10},{16,20},{18,... | collective-permute-start | bytes 3145736 | tf_op jit(solution)/shard_map/ppermute | solution.py:1029
  161.4 25.6 %collective-permute-start.30 = (bf16[2,4,128,512]{3,2,1,0:T(8,128)(2,1)}, bf16[2,4,128,512]{3,2,1,0:T(8,128)(2,1)}, u32[]{:S(2)}, u32[]{:S(2)}) collective-permute-start(bf16[2,4,128,512]{3,2,1,0:T(8,128)(2,1)} %pad_maximum_fusion.3.refs_1_), channel_id=1, source_target_pairs={{0,1},{1,0},{2,3},{3,2},{4,5},{5,4},{6,7},{7,6},{8,9},{9,8},{10,11... | collective-permute-start | bytes 3145736 | tf_op jit(solution)/shard_map/ppermute | solution.py:1023
  162.6 24.9 %collective-permute-start.32 = (bf16[2,4,128,512]{3,2,1,0:T(8,128)(2,1)}, bf16[2,4,128,512]{3,2,1,0:T(8,128)(2,1)}, u32[]{:S(2)}, u32[]{:S(2)}) collective-permute-start(bf16[2,4,128,512]{3,2,1,0:T(8,128)(2,1)} %pad_maximum_fusion.2.refs_0_), channel_id=1, source_target_pairs={{0,2},{2,0},{4,6},{6,4},{8,10},{10,8},{12,14},{14,12},{16,18},{18,... | collective-permute-start | bytes 3145736 | tf_op jit(solution)/shard_map/ppermute | solution.py:1029
  162.7 24.8 %collective-permute-start.33 = (bf16[2,4,128,512]{3,2,1,0:T(8,128)(2,1)}, bf16[2,4,128,512]{3,2,1,0:T(8,128)(2,1)}, u32[]{:S(2)}, u32[]{:S(2)}) collective-permute-start(bf16[2,4,128,512]{3,2,1,0:T(8,128)(2,1)} %pad_maximum_fusion.3.refs_1_), channel_id=1, source_target_pairs={{0,2},{2,0},{4,6},{6,4},{8,10},{10,8},{12,14},{14,12},{16,18},{18,... | collective-permute-start | bytes 3145736 | tf_op jit(solution)/shard_map/ppermute | solution.py:1029
  187.0 4.4 %collective-permute-start.35 = (bf16[2,4,128,512]{3,2,1,0:T(8,128)(2,1)}, bf16[2,4,128,512]{3,2,1,0:T(8,128)(2,1)S(1)}, u32[]{:S(2)}, u32[]{:S(2)}) collective-permute-start(bf16[2,4,128,512]{3,2,1,0:T(8,128)(2,1)} %collective-permute-done.30.refs_3_), channel_id=1, source_target_pairs={{0,2},{2,0},{4,6},{6,4},{8,10},{10,8},{12,14},{14,12},{16,18},{18,... | collective-permute-start | bytes 3145736 | tf_op jit(solution)/shard_map/ppermute | solution.py:1029
  191.4 14.5 %collective-permute-start.36 = (bf16[680,4096]{1,0:T(8,128)(2,1)}, bf16[680,4096]{1,0:T(8,128)(2,1)}, u32[]{:S(2)}, u32[]{:S(2)}) collective-permute-start(bf16[680,4096]{1,0:T(8,128)(2,1)} %get-tuple-element.616.own_ref.x_ref), channel_id=1, source_target_pairs={{0,2},{2,0},{4,6},{6,4},{8,10},{10,8},{12,14},{14,12},{16,18},{18,... | collective-permute-start | bytes 16711688 | tf_op jit(solution)/shard_map/ppermute | solution.py:988
  191.5 14.3 %collective-permute-start.38 = (bf16[680,1024]{1,0:T(8,128)(2,1)S(1)}, bf16[680,1024]{1,0:T(8,128)(2,1)}, u32[]{:S(2)}, u32[]{:S(2)}) collective-permute-start(bf16[680,1024]{1,0:T(8,128)(2,1)S(1)} %copy-done.5), channel_id=1, source_target_pairs={{0,2},{2,0},{4,6},{6,4},{8,10},{10,8},{12,14},{14,12},{16,18},{18,... | collective-permute-start | bytes 4177928 | tf_op jit(solution)/shard_map/ppermute | solution.py:988
  191.9 13.9 %collective-permute-start.39 = (bf16[680,1024]{1,0:T(8,128)(2,1)S(1)}, bf16[680,1024]{1,0:T(8,128)(2,1)}, u32[]{:S(2)}, u32[]{:S(2)}) collective-permute-start(bf16[680,1024]{1,0:T(8,128)(2,1)S(1)} %copy-done.28), channel_id=1, source_target_pairs={{0,2},{2,0},{4,6},{6,4},{8,10},{10,8},{12,14},{14,12},{16,18},{18,... | collective-permute-start | bytes 4177928 | tf_op jit(solution)/shard_map/ppermute | solution.py:988
  192.4 13.5 %collective-permute-start.37 = (bf16[680,512]{1,0:T(8,128)(2,1)}, bf16[680,512]{1,0:T(8,128)(2,1)}, u32[]{:S(2)}, u32[]{:S(2)}) collective-permute-start(bf16[680,512]{1,0:T(8,128)(2,1)} %constant_dynamic-slice_fusion), channel_id=1, source_target_pairs={{0,2},{2,0},{4,6},{6,4},{8,10},{10,8},{12,14},{14,12},{16,18},{18,... | collective-permute-start | bytes 2088968 | tf_op jit(solution)/shard_map/ppermute | solution.py:988
  205.9 38.0 %collective-permute-start.42 = (bf16[680,2048]{1,0:T(8,128)(2,1)}, bf16[680,2048]{1,0:T(8,128)(2,1)}, u32[]{:S(2)}, u32[]{:S(2)}) collective-permute-start(bf16[680,2048]{1,0:T(8,128)(2,1)} %get-tuple-element.505), channel_id=1, source_target_pairs={{0,2},{2,0},{4,6},{6,4},{8,10},{10,8},{12,14},{14,12},{16,18},{18,... | collective-permute-start | bytes 8355848 | tf_op jit(solution)/shard_map/ppermute | solution.py:988
  218.2 25.4 %collective-permute-start.40 = (bf16[2,4,2,128,256]{4,3,2,1,0:T(8,128)(2,1)}, bf16[2,4,2,128,256]{4,3,2,1,0:T(8,128)(2,1)S(1)}, u32[]{:S(2)}, u32[]{:S(2)}) collective-permute-start(bf16[2,4,2,128,256]{4,3,2,1,0:T(8,128)(2,1)} %get-tuple-element.503), channel_id=1, source_target_pairs={{0,1},{1,0},{2,3},{3,2},{4,5},{5,4},{6,7},{7,6},{8,9},{9,8},{10,11... | collective-permute-start | bytes 3145736 | tf_op jit(solution)/shard_map/ppermute | solution.py:1023
  218.7 25.1 %collective-permute-start.41 = (bf16[2,4,2,128,256]{4,3,2,1,0:T(8,128)(2,1)}, bf16[2,4,2,128,256]{4,3,2,1,0:T(8,128)(2,1)S(1)}, u32[]{:S(2)}, u32[]{:S(2)}) collective-permute-start(bf16[2,4,2,128,256]{4,3,2,1,0:T(8,128)(2,1)} %get-tuple-element.504), channel_id=1, source_target_pairs={{0,4},{2,6},{4,0},{6,2},{8,12},{10,14},{12,8},{14,10},{16,20},{18,... | collective-permute-start | bytes 3145736 | tf_op jit(solution)/shard_map/ppermute | solution.py:1029
  239.5 9.3 %collective-permute-start.43 = (bf16[680,512]{1,0:T(8,128)(2,1)S(1)}, bf16[680,512]{1,0:T(8,128)(2,1)}, u32[]{:S(2)}, u32[]{:S(2)}) collective-permute-start(bf16[680,512]{1,0:T(8,128)(2,1)S(1)} %get-tuple-element.516), channel_id=1, source_target_pairs={{0,2},{2,0},{4,6},{6,4},{8,10},{10,8},{12,14},{14,12},{16,18},{18,... | collective-permute-start | bytes 2088968 | tf_op jit(solution)/shard_map/ppermute | solution.py:988
  246.5 20.1 %collective-permute-start.44 = (bf16[4,2,128,256]{3,2,1,0:T(8,128)(2,1)}, bf16[4,2,128,256]{3,2,1,0:T(8,128)(2,1)}, u32[]{:S(2)}, u32[]{:S(2)}) collective-permute-start(bf16[4,2,128,256]{3,2,1,0:T(8,128)(2,1)} %get-tuple-element.518), channel_id=1, source_target_pairs={{0,4},{2,6},{4,0},{6,2},{8,12},{10,14},{12,8},{14,10},{16,20},{18,... | collective-permute-start | bytes 1572872 | tf_op jit(solution)/shard_map/ppermute | solution.py:1029
  247.3 19.4 %collective-permute-start.45 = (bf16[4,2,128,256]{3,2,1,0:T(8,128)(2,1)}, bf16[4,2,128,256]{3,2,1,0:T(8,128)(2,1)}, u32[]{:S(2)}, u32[]{:S(2)}) collective-permute-start(bf16[4,2,128,256]{3,2,1,0:T(8,128)(2,1)} %get-tuple-element.519), channel_id=1, source_target_pairs={{0,1},{1,0},{2,3},{3,2},{4,5},{5,4},{6,7},{7,6},{8,9},{9,8},{10,11... | collective-permute-start | bytes 1572872 | tf_op jit(solution)/shard_map/ppermute | solution.py:1023
  266.7 39.6 %collective-permute-start.47 = (bf16[2,4,2,32,1280]{4,3,2,1,0:T(8,128)(2,1)}, bf16[2,4,2,32,1280]{4,3,2,1,0:T(8,128)(2,1)S(1)}, u32[]{:S(2)}, u32[]{:S(2)}) collective-permute-start(bf16[2,4,2,32,1280]{4,3,2,1,0:T(8,128)(2,1)} %get-tuple-element.540), channel_id=1, source_target_pairs={{0,1},{1,0},{2,3},{3,2},{4,5},{5,4},{6,7},{7,6},{8,9},{9,8},{10,11... | collective-permute-start | bytes 3932168 | tf_op jit(solution)/shard_map/ppermute | solution.py:1023
  267.3 39.0 %collective-permute-start.48 = (bf16[2,4,2,32,1280]{4,3,2,1,0:T(8,128)(2,1)}, bf16[2,4,2,32,1280]{4,3,2,1,0:T(8,128)(2,1)S(1)}, u32[]{:S(2)}, u32[]{:S(2)}) collective-permute-start(bf16[2,4,2,32,1280]{4,3,2,1,0:T(8,128)(2,1)} %get-tuple-element.541), channel_id=1, source_target_pairs={{0,4},{2,6},{4,0},{6,2},{8,12},{10,14},{12,8},{14,10},{16,20},{18,... | collective-permute-start | bytes 3932168 | tf_op jit(solution)/shard_map/ppermute | solution.py:1029
  270.6 35.7 %collective-permute-start.46 = (bf16[2,2,128,512]{3,2,1,0:T(8,128)(2,1)S(1)}, bf16[2,2,128,512]{3,2,1,0:T(8,128)(2,1)S(1)}, u32[]{:S(2)}, u32[]{:S(2)}) collective-permute-start(bf16[2,2,128,512]{3,2,1,0:T(8,128)(2,1)S(1)} %get-tuple-element.539), channel_id=1, source_target_pairs={{0,8},{2,10},{4,12},{6,14},{8,0},{10,2},{12,4},{14,6},{16,24},{18,... | collective-permute-start | bytes 1572872 | tf_op jit(solution)/shard_map/ppermute | solution.py:1029
  306.3 9.8 %collective-permute-start.49 = (bf16[680,1536]{1,0:T(8,128)(2,1)S(1)}, bf16[680,1536]{1,0:T(8,128)(2,1)}, u32[]{:S(2)}, u32[]{:S(2)}) collective-permute-start(bf16[680,1536]{1,0:T(8,128)(2,1)S(1)} %get-tuple-element.562), channel_id=1, source_target_pairs={{0,2},{2,0},{4,6},{6,4},{8,10},{10,8},{12,14},{14,12},{16,18},{18,... | collective-permute-start | bytes 6266888 | tf_op jit(solution)/shard_map/ppermute | solution.py:988
  310.1 18.3 %collective-permute-start.51 = (bf16[4,2,32,1280]{3,2,1,0:T(8,128)(2,1)}, bf16[4,2,32,1280]{3,2,1,0:T(8,128)(2,1)}, u32[]{:S(2)}, u32[]{:S(2)}) collective-permute-start(bf16[4,2,32,1280]{3,2,1,0:T(8,128)(2,1)} %get-tuple-element.565), channel_id=1, source_target_pairs={{0,4},{2,6},{4,0},{6,2},{8,12},{10,14},{12,8},{14,10},{16,20},{18,... | collective-permute-start | bytes 1966088 | tf_op jit(solution)/shard_map/ppermute | solution.py:1029
  311.3 17.1 %collective-permute-start.52 = (bf16[4,2,32,1280]{3,2,1,0:T(8,128)(2,1)}, bf16[4,2,32,1280]{3,2,1,0:T(8,128)(2,1)}, u32[]{:S(2)}, u32[]{:S(2)}) collective-permute-start(bf16[4,2,32,1280]{3,2,1,0:T(8,128)(2,1)} %get-tuple-element.566), channel_id=1, source_target_pairs={{0,1},{1,0},{2,3},{3,2},{4,5},{5,4},{6,7},{7,6},{8,9},{9,8},{10,11... | collective-permute-start | bytes 1966088 | tf_op jit(solution)/shard_map/ppermute | solution.py:1023
  314.1 14.3 %collective-permute-start.50 = (bf16[2,128,512]{2,1,0:T(8,128)(2,1)}, bf16[2,128,512]{2,1,0:T(8,128)(2,1)S(1)}, u32[]{:S(2)}, u32[]{:S(2)}) collective-permute-start(bf16[2,128,512]{2,1,0:T(8,128)(2,1)} %bitcast.44), channel_id=1, source_target_pairs={{0,16},{2,18},{4,20},{6,22},{8,24},{10,26},{12,28},{14,30},{16,0},... | collective-permute-start | bytes 786440 | tf_op jit(solution)/shard_map/ppermute | solution.py:1029
  328.4 24.5 %collective-permute-start.53 = (bf16[2,4,2,32,768]{4,3,2,1,0:T(8,128)(2,1)}, bf16[2,4,2,32,768]{4,3,2,1,0:T(8,128)(2,1)S(1)}, u32[]{:S(2)}, u32[]{:S(2)}) collective-permute-start(bf16[2,4,2,32,768]{4,3,2,1,0:T(8,128)(2,1)} %get-tuple-element.594), channel_id=1, source_target_pairs={{0,1},{1,0},{2,3},{3,2},{4,5},{5,4},{6,7},{7,6},{8,9},{9,8},{10,11... | collective-permute-start | bytes 2359304 | tf_op jit(solution)/shard_map/ppermute | solution.py:1023
  329.4 23.6 %collective-permute-start.54 = (bf16[2,4,2,32,768]{4,3,2,1,0:T(8,128)(2,1)}, bf16[2,4,2,32,768]{4,3,2,1,0:T(8,128)(2,1)S(1)}, u32[]{:S(2)}, u32[]{:S(2)}) collective-permute-start(bf16[2,4,2,32,768]{4,3,2,1,0:T(8,128)(2,1)} %get-tuple-element.595), channel_id=1, source_target_pairs={{0,4},{2,6},{4,0},{6,2},{8,12},{10,14},{12,8},{14,10},{16,20},{18,... | collective-permute-start | bytes 2359304 | tf_op jit(solution)/shard_map/ppermute | solution.py:1029
  333.5 19.5 %collective-permute-start.55 = (bf16[2,2,32,2560]{3,2,1,0:T(8,128)(2,1)S(1)}, bf16[2,2,32,2560]{3,2,1,0:T(8,128)(2,1)S(1)}, u32[]{:S(2)}, u32[]{:S(2)}) collective-permute-start(bf16[2,2,32,2560]{3,2,1,0:T(8,128)(2,1)S(1)} %get-tuple-element.596), channel_id=1, source_target_pairs={{0,8},{2,10},{4,12},{6,14},{8,0},{10,2},{12,4},{14,6},{16,24},{18,... | collective-permute-start | bytes 1966088 | tf_op jit(solution)/shard_map/ppermute | solution.py:1029
  354.2 18.8 %collective-permute-start.56 = (bf16[4,2,32,768]{3,2,1,0:T(8,128)(2,1)S(1)}, bf16[4,2,32,768]{3,2,1,0:T(8,128)(2,1)S(1)}, u32[]{:S(2)}, u32[]{:S(2)}) collective-permute-start(bf16[4,2,32,768]{3,2,1,0:T(8,128)(2,1)S(1)} %get-tuple-element.613), channel_id=1, source_target_pairs={{0,4},{2,6},{4,0},{6,2},{8,12},{10,14},{12,8},{14,10},{16,20},{18,... | collective-permute-start | bytes 1179656 | tf_op jit(solution)/shard_map/ppermute | solution.py:1029
  354.9 18.0 %collective-permute-start.57 = (bf16[4,2,32,768]{3,2,1,0:T(8,128)(2,1)S(1)}, bf16[4,2,32,768]{3,2,1,0:T(8,128)(2,1)S(1)}, u32[]{:S(2)}, u32[]{:S(2)}) collective-permute-start(bf16[4,2,32,768]{3,2,1,0:T(8,128)(2,1)S(1)} %get-tuple-element.614), channel_id=1, source_target_pairs={{0,1},{1,0},{2,3},{3,2},{4,5},{5,4},{6,7},{7,6},{8,9},{9,8},{10,11... | collective-permute-start | bytes 1179656 | tf_op jit(solution)/shard_map/ppermute | solution.py:1023
  356.8 16.2 %collective-permute-start.58 = (bf16[2,32,2560]{2,1,0:T(8,128)(2,1)S(1)}, bf16[2,32,2560]{2,1,0:T(8,128)(2,1)S(1)}, u32[]{:S(2)}, u32[]{:S(2)}) collective-permute-start(bf16[2,32,2560]{2,1,0:T(8,128)(2,1)S(1)} %bitcast.126), channel_id=1, source_target_pairs={{0,16},{2,18},{4,20},{6,22},{8,24},{10,26},{12,28},{14,30},{16,0},... | collective-permute-start | bytes 983048 | tf_op jit(solution)/shard_map/ppermute | solution.py:1029
  359.5 28.3 %collective-permute-start.61 = (f32[128,512]{1,0:T(8,128)}, f32[128,512]{1,0:T(8,128)}, u32[]{:S(2)}, u32[]{:S(2)}) collective-permute-start(f32[128,512]{1,0:T(8,128)} %bitcast.52), channel_id=1, source_target_pairs={{0,2},{2,0},{4,6},{6,4},{8,10},{10,8},{12,14},{14,12},{16,18},{18,... | collective-permute-start | bytes 786440 | tf_op jit(solution)/shard_map/ppermute | solution.py:1029
  375.0 11.1 %collective-permute-start.59 = (bf16[2,2,32,1536]{3,2,1,0:T(8,128)(2,1)S(1)}, bf16[2,2,32,1536]{3,2,1,0:T(8,128)(2,1)S(1)}, u32[]{:S(2)}, u32[]{:S(2)}) collective-permute-start(bf16[2,2,32,1536]{3,2,1,0:T(8,128)(2,1)S(1)} %get-tuple-element.637), channel_id=1, source_target_pairs={{0,8},{2,10},{4,12},{6,14},{8,0},{10,2},{12,4},{14,6},{16,24},{18,... | collective-permute-start | bytes 1179656 | tf_op jit(solution)/shard_map/ppermute | solution.py:1029
  375.1 12.8 %collective-permute-start.62 = (f32[32,2560]{1,0:T(8,128)}, f32[32,2560]{1,0:T(8,128)}, u32[]{:S(2)}, u32[]{:S(2)}) collective-permute-start(f32[32,2560]{1,0:T(8,128)} %bitcast.54), channel_id=1, source_target_pairs={{0,2},{2,0},{4,6},{6,4},{8,10},{10,8},{12,14},{14,12},{16,18},{18,... | collective-permute-start | bytes 983048 | tf_op jit(solution)/shard_map/ppermute | solution.py:1029
  386.2 8.5 %collective-permute-start.64 = (bf16[2,48,128]{2,1,0:T(8,128)(2,1)S(1)}, bf16[2,48,128]{2,1,0:T(8,128)(2,1)S(1)}, u32[]{:S(2)}, u32[]{:S(2)}) collective-permute-start(bf16[2,48,128]{2,1,0:T(8,128)(2,1)S(1)} %pad_maximum_fusion.23), channel_id=1, source_target_pairs={{0,4},{2,6},{4,0},{6,2},{8,12},{10,14},{12,8},{14,10},{16,20},{18,... | collective-permute-start | bytes 73736 | tf_op jit(solution)/shard_map/ppermute | solution.py:1029
  387.9 11.2 %collective-permute-start.63 = (bf16[2,32,1536]{2,1,0:T(8,128)(2,1)S(1)}, bf16[2,32,1536]{2,1,0:T(8,128)(2,1)S(1)}, u32[]{:S(2)}, u32[]{:S(2)}) collective-permute-start(bf16[2,32,1536]{2,1,0:T(8,128)(2,1)S(1)} %bitcast.127), channel_id=1, source_target_pairs={{0,16},{2,18},{4,20},{6,22},{8,24},{10,26},{12,28},{14,30},{16,0},... | collective-permute-start | bytes 589832 | tf_op jit(solution)/shard_map/ppermute | solution.py:1029
  401.2 7.6 %collective-permute-start.65 = (f32[32,1536]{1,0:T(8,128)S(1)}, f32[32,1536]{1,0:T(8,128)S(1)}, u32[]{:S(2)}, u32[]{:S(2)}) collective-permute-start(f32[32,1536]{1,0:T(8,128)S(1)} %bitcast.128), channel_id=1, source_target_pairs={{0,2},{2,0},{4,6},{6,4},{8,10},{10,8},{12,14},{14,12},{16,18},{18,... | collective-permute-start | bytes 589832 | tf_op jit(solution)/shard_map/ppermute | solution.py:1029
  403.1 5.6 %collective-permute-start.67 = (bf16[2,2,2,48,128]{4,3,2,1,0:T(8,128)(2,1)S(1)}, bf16[2,2,2,48,128]{4,3,2,1,0:T(8,128)(2,1)S(1)}, u32[]{:S(2)}, u32[]{:S(2)}) collective-permute-start(bf16[2,2,2,48,128]{4,3,2,1,0:T(8,128)(2,1)S(1)} %get-tuple-element.727), channel_id=1, source_target_pairs={{0,16},{2,18},{4,20},{6,22},{8,24},{10,26},{12,28},{14,30},{16,0},... | collective-permute-start | bytes 294920 | tf_op jit(solution)/shard_map/ppermute | solution.py:1029
  408.8 5.7 %collective-permute-start.68 = (bf16[2,2,2,2,48,128]{5,4,3,2,1,0:T(8,128)(2,1)S(1)}, bf16[2,2,2,2,48,128]{5,4,3,2,1,0:T(8,128)(2,1)S(1)}, u32[]{:S(2)}, u32[]{:S(2)}) collective-permute-start(bf16[2,2,2,2,48,128]{5,4,3,2,1,0:T(8,128)(2,1)S(1)} %get-tuple-element.725), channel_id=1, source_target_pairs={{0,8},{2,10},{4,12},{6,14},{8,0},{10,2},{12,4},{14,6},{16,24},{18,... | collective-permute-start | bytes 589832 | tf_op jit(solution)/shard_map/ppermute | solution.py:1029
  (76 other events, 703.6 us)
where the time goes:
time: 424 us; the launch traced here: 418 us
  Pallas kernels  222 us (52%)
  waiting for transfers between devices  77.4 us (18%)
  starting transfers between devices  63 us (15%)
  other arithmetic  33.9 us (8%)
  local copies, waits for them, and re-layouts  14.2 us (3%)
    ppermute x47, waiting for transfers between devices, flip(): return lax.ppermute(array, 'fsdp', pairs)  60.6 us
    pallas_call x4, Pallas kernels, gather_dot(): pl.pallas_call(functools.partial(gather_kernel, (rows, left, half, chunk,...  47.7 us
    ppermute x47, starting transfers between devices, flip(): return lax.ppermute(array, 'fsdp', pairs)  39.5 us
    pallas_call x2, Pallas kernels, modulate_back(): pl.pallas_call(functools.partial(modulate_back_kernel, depth // chunk, mo...  36.7 us
    pallas_call x2, Pallas kernels, attend_forward(): pl.pallas_call(kernel, grid=(end - begin,), in_specs=[block(0), block(pai...  34.6 us
    pallas_call x1, Pallas kernels, attend_backward(): pl.pallas_call(functools.partial(attend_back_kernel, half), grid_spec=plt...  31.8 us
    pallas_call x2, Pallas kernels, weight_grad_call(): pl.pallas_call(functools.partial(weight_grad_kernel, depth, rows, turn, t...  28.9 us
    pallas_call x12, Pallas kernels, add_split(): pl.pallas_call(functools.partial(add_split_kernel, joined), grid_spec=plt...  17.4 us
  transfers between devices with their start and end apart: 70, of which 28 were waited for; matrix products, arithmetic and copies ran while one was open for 7% of the time, Pallas kernels for 53%

commit v1 on v0

--- a/solution.py
+++ b/solution.py
@@ -1207,17 +1207,17 @@
     else:
         wide_proj = lax.all_gather(cast_proj, AXES, axis=0, tiled=True)
         attended = jnp.dot(context, wide_proj, preferred_element_type=f32)
-    if fits:
-        attended = line.arrive([all_fc2], attended)
-        all_fc2.fourth()
-        attended = line(attended)
     middle = tokens + gamma_one * attended
     second, modulate_two = jax.vjp(modulate, middle, scale_two, shift_two)
-    if not fits:
+    second_low = second.astype(bf16)
+    if fits:
+        second_low = line.arrive([all_fc2], second_low)
+        all_fc2.fourth()
+    else:
         upstream = cotangent[0].astype(f32) * valid
         d_branch = (upstream * gamma_two).astype(bf16)
         give = half_columns(d_branch, 1 - here["c"])
-    second_low = line(second.astype(bf16))
+    second_low = line(second_low)
     second_other = grid.shift(second_low, "c", 1)
     if fits:
         wide_fc1, slope, activated_low = gather_dot(

time: 424 us -> 423 us (level)
    unnamed x145 -> x143, local copies, waits for them, and re-layouts: 9.67 us -> 9.66 us
  transfers between devices with their start and end apart: 70 -> 70, of which waited for: 28 -> 26; matrix products, arithmetic and copies ran while one was open for 7% -> 8% of each run, Pallas kernels for 53% -> 53%
where the time goes in v1:
time: 423 us; the launch traced here: 418 us
  Pallas kernels  222 us (52%)
  waiting for transfers between devices  75.1 us (18%)
  starting transfers between devices  63.2 us (15%)
  other arithmetic  35.7 us (8%)
  local copies, waits for them, and re-layouts  14.2 us (3%)
    ppermute x47, waiting for transfers between devices, flip(): return lax.ppermute(array, 'fsdp', pairs)  59.4 us
    pallas_call x4, Pallas kernels, gather_dot(): pl.pallas_call(functools.partial(gather_kernel, (rows, left, half, chunk,...  47.7 us
    ppermute x47, starting transfers between devices, flip(): return lax.ppermute(array, 'fsdp', pairs)  39.7 us
    pallas_call x2, Pallas kernels, modulate_back(): pl.pallas_call(functools.partial(modulate_back_kernel, depth // chunk, mo...  36.7 us
    pallas_call x2, Pallas kernels, attend_forward(): pl.pallas_call(kernel, grid=(end - begin,), in_specs=[block(0), block(pai...  34.6 us
    pallas_call x1, Pallas kernels, attend_backward(): pl.pallas_call(functools.partial(attend_back_kernel, half), grid_spec=plt...  31.8 us
    pallas_call x2, Pallas kernels, weight_grad_call(): pl.pallas_call(functools.partial(weight_grad_kernel, depth, rows, turn, t...  28.8 us
    pallas_call x12, Pallas kernels, add_split(): pl.pallas_call(functools.partial(add_split_kernel, joined), grid_spec=plt...  17.4 us
  transfers between devices with their start and end apart: 70, of which 26 were waited for; matrix products, arithmetic and copies ran while one was open for 8% of the time, Pallas kernels for 53%

profile of v1, /device:TPU:0, one launch (start us, length us, event | category | flops | bytes accessed | tf_op | source)
XLA Modules:
  0.0 418.1 jit_solution(14749250487886868772)
XLA Ops:
  2.0 7.3 %all-to-all-start = ((s32[32,1,1]{2,1,0:T(1,128)}), s32[32,1,1]{2,1,0:T(1,128)S(1)}, u32[]{:S(2)}, u32[]{:S(2)}) async-start(s32[32,1,1]{2,1,0:T(1,128)} %broadcast_in_dim.121), calls=%async_computation | async-start | bytes 32768 | tf_op jit(solution)/shard_map/all_to_all | solution.py:1090
  10.4 2.7 collective-permute-start.1
  23.1 1.5 collective-permute-start.2
  24.6 1.5 collective-permute-start.3
  26.2 3.9 collective-permute-done.2
  30.1 5.4 %collective-permute-done.3 = bf16[2,32,3072]{2,1,0:T(8,128)(2,1)S(1)} collective-permute-done((bf16[2,32,3072]{2,1,0:T(8,128)(2,1)S(1)}, bf16[2,32,3072]{2,1,0:T(8,128)(2,1)S(1)}, u32[]{:S(2)}, u32[]{:S(2)}) %collective-permute-start.3) | collective-permute-done | bytes 393248 | tf_op jit(solution)/shard_map/ppermute | solution.py:1029
  35.6 1.6 collective-permute-start.4
  38.8 1.8 collective-permute-start.8
  41.4 7.1 %collective-permute-done.5 = bf16[4,32,1536]{2,1,0:T(8,128)(2,1)S(1)} collective-permute-done((bf16[4,32,1536]{2,1,0:T(8,128)(2,1)S(1)}, bf16[4,32,1536]{2,1,0:T(8,128)(2,1)S(1)}, u32[]{:S(2)}, u32[]{:S(2)}) %collective-permute-start.5) | collective-permute-done | bytes 393248 | tf_op jit(solution)/shard_map/ppermute | solution.py:1023
  48.7 2.1 collective-permute-start.7
  52.1 4.0 collective-permute-done.8
  56.1 1.5 collective-permute-start.9
  58.4 2.2 and_select_fusion
  60.6 12.6 %collective-permute-done.11 = bf16[2,32,5120]{2,1,0:T(8,128)(2,1)S(1)} collective-permute-done((bf16[2,32,5120]{2,1,0:T(8,128)(2,1)S(1)}, bf16[2,32,5120]{2,1,0:T(8,128)(2,1)S(1)}, u32[]{:S(2)}, u32[]{:S(2)}) %collective-permute-start.11) | collective-permute-done | bytes 655392 | tf_op jit(solution)/shard_map/ppermute | solution.py:1029
  75.3 1.7 collective-permute-done.14
  77.0 1.5 collective-permute-start.17
  78.5 1.3 collective-permute-start.18
  79.8 1.7 fusion.5.x_ref.refs_0_
  82.4 11.2 %gather_qkv.1 = (bf16[1024,3072]{1,0:T(8,128)(2,1)}, bf16[680,3072]{1,0:T(8,128)(2,1)}) custom-call(s32[5]{0:T(128)} %stack.50.place_ref, bf16[680,1024]{1,0:T(8,128)(2,1)} %fusion.5.x_ref.refs_0_, bf16[2,4,32,1536]{3,2,1,0:T(8,128)(2,1)} %copy-done.40, bf16[2,4,32,1536]{3,2,1,0:T(8,128)(2,1)} %copy-done.39, bf16[2,4,32,1536]{3,2,1,0:T(8,128)(2,1)} %copy-done.50, ...), custom_call_target="tpu_custom_call" | custom-call | flops 100270080 | bytes 228864 | tf_op jit(solution)/shard_map/gather_qkv/pallas_call | solution.py:346
  93.7 1.5 pad_maximum_fusion.1.refs_1_
  95.2 2.0 pad_maximum_fusion.refs_0_
  99.0 3.3 collective-permute-start.19
  102.3 11.0 %attend.2 = (bf16[680,1024]{1,0:T(8,128)(2,1)S(1)}, f32[8,2,680]{2,1,0:T(2,128)S(1)}) custom-call(bf16[680,3072]{1,0:T(8,128)(2,1)S(1)} %copy-done, bf16[680,3072]{1,0:T(8,128)(2,1)S(1)} %copy-done, bf16[680,3072]{1,0:T(8,128)(2,1)S(1)} %copy-done, f32[680,680]{1,0:T(8,128)S(1)} %get-tuple-element.414.bias_ref), custom_call_target="tpu_custom_call" | custom-call | flops 36992000 | bytes 65280 | tf_op jit(solution)/shard_map/attend/pallas_call | solution.py:129
  114.7 23.6 %attend.3 = (bf16[680,1024]{1,0:T(8,128)(2,1)S(1)}, f32[8,2,680]{2,1,0:T(2,128)S(1)}) custom-call(bf16[680,3072]{1,0:T(8,128)(2,1)S(1)} %copy-done, bf16[680,3072]{1,0:T(8,128)(2,1)S(1)} %copy-done, bf16[680,3072]{1,0:T(8,128)(2,1)S(1)} %copy-done, f32[680,680]{1,0:T(8,128)S(1)} %get-tuple-element.414.bias_ref, ...), custom_call_target="tpu_custom_call", output_to_operand_aliasing={{0}: (4, {}), {1}: (5, {})} | custom-call | flops 36992000 | bytes 65280 | tf_op jit(solution)/shard_map/attend/pallas_call | solution.py:129
  140.2 1.6 collective-permute-start.27
  145.5 6.8 %gather_proj.1 = (bf16[1024,1024]{1,0:T(8,128)(2,1)}, f32[680,1024]{1,0:T(8,128)}) custom-call(s32[5]{0:T(128)} %stack.50.place_ref, bf16[680,1024]{1,0:T(8,128)(2,1)} %copy-done.4, bf16[2,4,32,2560]{3,2,1,0:T(8,128)(2,1)} %copy-done.30, bf16[2,4,32,2560]{3,2,1,0:T(8,128)(2,1)} %copy-done.29, bf16[2,4,32,2560]{3,2,1,0:T(8,128)(2,1)} %copy-done.33, ...), custom_call_target="tpu_custom_call" | custom-call | flops 33423360 | bytes 76288 | tf_op jit(solution)/shard_map/gather_proj/pallas_call | solution.py:346
  152.2 2.2 fusion.54
  154.9 1.6 add_convert_fusion.x_ref.refs_0_
  158.9 1.3 collective-permute-start.29
  160.2 1.5 collective-permute-start.30
  162.9 16.9 %gather_fc1.1 = (bf16[1024,4096]{1,0:T(8,128)(2,1)}, bf16[680,4096]{1,0:T(8,128)(2,1)}, bf16[680,4096]{1,0:T(8,128)(2,1)}) custom-call(s32[5]{0:T(128)} %stack.50.place_ref, bf16[680,1024]{1,0:T(8,128)(2,1)} %add_convert_fusion.x_ref.refs_0_, bf16[2,4,32,2560]{3,2,1,0:T(8,128)(2,1)} %copy-done.30, bf16[2,4,32,2560]{3,2,1,0:T(8,128)(2,1)} %copy-done.29, ...), custom_call_target="tpu_custom_call" | custom-call | flops 133693440 | bytes 305152 | tf_op jit(solution)/shard_map/gather_fc1/pallas_call | solution.py:346
  181.2 3.4 collective-permute-done.29.refs_2_
  186.2 2.4 collective-permute-done.34.refs_6_
  188.5 1.5 collective-permute-done.35.refs_7_
  191.2 13.1 %gelu_back.1 = (bf16[680,4096]{1,0:T(8,128)(2,1)}, bf16[680,2048]{1,0:T(8,128)(2,1)}) custom-call(s32[5]{0:T(128)} %stack.50.place_ref, bf16[680,1024]{1,0:T(8,128)(2,1)} %copy-done.27, bf16[680,4096]{1,0:T(8,128)(2,1)} %get-tuple-element.469.slope_ref, bf16[2,4,128,512]{3,2,1,0:T(8,128)(2,1)} %pad_maximum_fusion.2.refs_0_, ...), custom_call_target="tpu_custom_call" | custom-call | flops 133693440 | bytes 610304 | tf_op jit(solution)/shard_map/gelu_back/pallas_call | solution.py:580
  205.0 11.7 %weight_grad_rows.1 = (bf16[2,4,2,128,256]{4,3,2,1,0:T(8,128)(2,1)}, bf16[2,4,2,128,256]{4,3,2,1,0:T(8,128)(2,1)}, bf16[2,4,2,128,256]{4,3,2,1,0:T(8,128)(2,1)}, bf16[2,4,2,128,256]{4,3,2,1,0:T(8,128)(2,1)}) custom-call(s32[5]{0:T(128)} %stack.50.place_ref, bf16[680,4096]{1,0:T(8,128)(2,1)} %get-tuple-element.612.own_ref.x_ref, ...), custom_call_target="tpu_custom_call" | custom-call | flops 89128960 | bytes 261376 | tf_op jit(solution)/shard_map/weight_grad_rows/pallas_call | solution.py:731
  216.7 1.5 collective-permute-start.40
  219.1 19.9 %modulate_back.2 = (f32[680,1024]{1,0:T(8,128)}, bf16[680,1024]{1,0:T(8,128)(2,1)S(1)}, bf16[680,512]{1,0:T(8,128)(2,1)S(1)}, bf16[680,1024]{1,0:T(8,128)(2,1)S(1)}, f32[8,1024]{1,0:T(8,128)S(1)}) custom-call(s32[5]{0:T(128)S(1)} %copy-done.21, bf16[680,4096]{1,0:T(8,128)(2,1)} %get-tuple-element.490.x_ref.refs_2_, ...), custom_call_target="tpu_custom_call" | custom-call | flops 167116800 | bytes 392192 | tf_op jit(solution)/shard_map/modulate_back/pallas_call | solution.py:489
  239.1 3.2 collective-permute-done.40.refs_1_.refs_3_
  243.5 2.6 add_second.3
  247.4 17.8 %weight_grad.2 = (bf16[2,4,2,32,1280]{4,3,2,1,0:T(8,128)(2,1)}, bf16[2,4,2,32,1280]{4,3,2,1,0:T(8,128)(2,1)}, bf16[2,4,2,32,1280]{4,3,2,1,0:T(8,128)(2,1)}, bf16[2,4,2,32,1280]{4,3,2,1,0:T(8,128)(2,1)}) custom-call(s32[5]{0:T(128)} %stack.50.place_ref, bf16[680,1024]{1,0:T(8,128)(2,1)} %add_convert_fusion.x_ref.refs_0_, ...), custom_call_target="tpu_custom_call" | custom-call | flops 167116800 | bytes 332160 | tf_op jit(solution)/shard_map/weight_grad/pallas_call | solution.py:685
  265.2 1.6 collective-permute-start.47
  268.1 2.0 add_third.3
  271.0 1.6 copy-done.8
  272.6 1.3 copy-done.20
  273.9 31.8 %attend_back.1 = (bf16[680,3072]{1,0:T(8,128)(2,1)S(1)}, bf16[680,1536]{1,0:T(8,128)(2,1)S(1)}) custom-call(s32[5]{0:T(128)S(1)} %copy-done.22, bf16[680,3072]{1,0:T(8,128)(2,1)S(1)} %copy-done.1, bf16[680,3072]{1,0:T(8,128)(2,1)S(1)} %copy-done.1, bf16[680,3072]{1,0:T(8,128)(2,1)S(1)} %copy-done.1, bf16[680,1024]{1,0:T(8,128)(2,1)S(1)} %copy-done.20, ...), custom_call_target="tpu_custom_call" | custom-call | flops 147968000 | bytes 174080 | tf_op jit(solution)/shard_map/attend_back/pallas_call | solution.py:236
  305.9 2.9 add_second.4
  312.7 1.9 collective-permute-start.50
  314.6 11.0 %weight_grad.3 = (bf16[2,4,2,32,768]{4,3,2,1,0:T(8,128)(2,1)}, bf16[2,4,2,32,768]{4,3,2,1,0:T(8,128)(2,1)}, bf16[2,4,2,32,768]{4,3,2,1,0:T(8,128)(2,1)}, bf16[2,4,2,32,768]{4,3,2,1,0:T(8,128)(2,1)}) custom-call(s32[5]{0:T(128)} %stack.50.place_ref, bf16[680,1024]{1,0:T(8,128)(2,1)} %fusion.5.x_ref.refs_0_, ...), custom_call_target="tpu_custom_call" | custom-call | flops 100270080 | bytes 190592 | tf_op jit(solution)/shard_map/weight_grad/pallas_call | solution.py:685
  325.6 1.4 collective-permute-done.50.refs_1_.refs_3_
  330.5 2.1 add_third.4
  334.8 16.9 %modulate_back.3 = (f32[680,1024]{1,0:T(8,128)}, f32[8,1024]{1,0:T(8,128)S(1)}) custom-call(s32[5]{0:T(128)S(1)} %copy-done.23, bf16[680,3072]{1,0:T(8,128)(2,1)} %copy-done.3, bf16[1024,3072]{1,0:T(8,128)(2,1)} %get-tuple-element.585.w_ref, f32[8,1024]{1,0:T(8,128)S(1)} %concatenate.96.rows_ref, bf16[680,1024]{1,0:T(8,128)(2,1)S(1)} %bitcast.114, ...), custom_call_target="tpu_custom_call" | custom-call | flops 100270080 | bytes 337664 | tf_op jit(solution)/shard_map/modulate_back/pallas_call | solution.py:489
  355.7 3.2 collective-permute-start.58
  359.1 12.8 %gather_fc2.1 = f32[680,1024]{1,0:T(8,128)} custom-call(s32[5]{0:T(128)} %stack.50.place_ref, bf16[680,4096]{1,0:T(8,128)(2,1)} %get-tuple-element.612.own_ref.x_ref, bf16[2,4,128,512]{3,2,1,0:T(8,128)(2,1)} %pad_maximum_fusion.2.refs_0_, bf16[2,4,128,512]{3,2,1,0:T(8,128)(2,1)} %pad_maximum_fusion.3.refs_1_, ...), custom_call_target="tpu_custom_call" | custom-call | flops 133693440 | bytes 174592 | tf_op jit(solution)/shard_map/gather_fc2/pallas_call | solution.py:346
  374.6 3.6 multiply_reduce_fusion
  379.5 6.1 %collective-permute-done.59.refs_1_.refs_3_ = bf16[2,2,32,1536]{3,2,1,0:T(8,128)(2,1)S(1)} collective-permute-done((bf16[2,2,32,1536]{3,2,1,0:T(8,128)(2,1)S(1)}, bf16[2,2,32,1536]{3,2,1,0:T(8,128)(2,1)S(1)}, u32[]{:S(2)}, u32[]{:S(2)}) %collective-permute-start.59) | collective-permute-done | bytes 393248 | tf_op jit(solution)/shard_map/ppermute | solution.py:1029
  389.6 2.7 fusion.46
  392.4 1.5 fusion.48
  393.9 4.7 %collective-permute-done.63.refs_1_.refs_3_ = bf16[2,32,1536]{2,1,0:T(8,128)(2,1)S(1)} collective-permute-done((bf16[2,32,1536]{2,1,0:T(8,128)(2,1)S(1)}, bf16[2,32,1536]{2,1,0:T(8,128)(2,1)S(1)}, u32[]{:S(2)}, u32[]{:S(2)}) %collective-permute-start.63) | collective-permute-done | bytes 196640 | tf_op jit(solution)/shard_map/ppermute | solution.py:1029
  399.7 3.0 collective-permute-done.66
  404.2 4.1 collective-permute-done.67
  408.6 2.1 fusion.52
  410.7 3.4 collective-permute-done.68
  414.4 2.3 fusion.44
  (342 shorter events, 67.3 us)
Async XLA Ops:
  2.0 17.0 %all-to-all-start = ((s32[32,1,1]{2,1,0:T(1,128)}), s32[32,1,1]{2,1,0:T(1,128)S(1)}, u32[]{:S(2)}, u32[]{:S(2)}) async-start(s32[32,1,1]{2,1,0:T(1,128)} %broadcast_in_dim.121), calls=%async_computation | async-start | bytes 32768 | tf_op jit(solution)/shard_map/all_to_all | solution.py:1090
  10.4 12.3 %collective-permute-start.1 = (bf16[32,3072]{1,0:T(8,128)(2,1)S(1)}, bf16[32,3072]{1,0:T(8,128)(2,1)S(1)}, u32[]{:S(2)}, u32[]{:S(2)}) collective-permute-start(bf16[32,3072]{1,0:T(8,128)(2,1)S(1)} %convert_element_type.75), channel_id=1, source_target_pairs={{0,16},{2,18},{4,20},{6,22},{8,24},{10,26},{12,28},{14,30},{16,0},... | collective-permute-start | bytes 589832 | tf_op jit(solution)/shard_map/ppermute | solution.py:1029
  23.1 7.0 %collective-permute-start.2 = (f32[2,2,2,48,128]{4,3,0,1,2:T(8,128)S(1)}, f32[2,2,2,48,128]{4,3,0,1,2:T(8,128)S(1)}, u32[]{:S(2)}, u32[]{:S(2)}) collective-permute-start(f32[2,2,2,48,128]{4,3,0,1,2:T(8,128)S(1)} %slice_bitcast_fusion), channel_id=1, source_target_pairs={{0,4},{2,6},{4,0},{6,2},{8,12},{10,14},{12,8},{14,10},{16,20},{18,... | collective-permute-start | bytes 589832 | tf_op jit(solution)/shard_map/ppermute | solution.py:1029
  24.6 10.9 %collective-permute-start.3 = (bf16[2,32,3072]{2,1,0:T(8,128)(2,1)S(1)}, bf16[2,32,3072]{2,1,0:T(8,128)(2,1)S(1)}, u32[]{:S(2)}, u32[]{:S(2)}) collective-permute-start(bf16[2,32,3072]{2,1,0:T(8,128)(2,1)S(1)} %pad_maximum_fusion.14), channel_id=1, source_target_pairs={{0,8},{2,10},{4,12},{6,14},{8,0},{10,2},{12,4},{14,6},{16,24},{18,... | collective-permute-start | bytes 1179656 | tf_op jit(solution)/shard_map/ppermute | solution.py:1029
  35.6 5.7 %collective-permute-start.4 = (f32[2,2,48,128]{3,2,0,1:T(8,128)S(1)}, f32[2,2,48,128]{3,2,0,1:T(8,128)S(1)}, u32[]{:S(2)}, u32[]{:S(2)}) collective-permute-start(f32[2,2,48,128]{3,2,0,1:T(8,128)S(1)} %slice_bitcast_fusion.2), channel_id=1, source_target_pairs={{0,1},{1,0},{2,3},{3,2},{4,5},{5,4},{6,7},{7,6},{8,9},{9,8},{10,11... | collective-permute-start | bytes 294920 | tf_op jit(solution)/shard_map/ppermute | solution.py:1023
  37.7 10.8 %collective-permute-start.5 = (bf16[4,32,1536]{2,1,0:T(8,128)(2,1)S(1)}, bf16[4,32,1536]{2,1,0:T(8,128)(2,1)S(1)}, u32[]{:S(2)}, u32[]{:S(2)}) collective-permute-start(bf16[4,32,1536]{2,1,0:T(8,128)(2,1)S(1)} %get-tuple-element.366), channel_id=1, source_target_pairs={{0,1},{1,0},{2,3},{3,2},{4,5},{5,4},{6,7},{7,6},{8,9},{9,8},{10,11... | collective-permute-start | bytes 1179656 | tf_op jit(solution)/shard_map/ppermute | solution.py:1023
  38.3 10.2 %collective-permute-start.6 = (bf16[4,32,1536]{2,1,0:T(8,128)(2,1)S(1)}, bf16[4,32,1536]{2,1,0:T(8,128)(2,1)S(1)}, u32[]{:S(2)}, u32[]{:S(2)}) collective-permute-start(bf16[4,32,1536]{2,1,0:T(8,128)(2,1)S(1)} %get-tuple-element.367), channel_id=1, source_target_pairs={{0,4},{2,6},{4,0},{6,2},{8,12},{10,14},{12,8},{14,10},{16,20},{18,... | collective-permute-start | bytes 1179656 | tf_op jit(solution)/shard_map/ppermute | solution.py:1029
  38.8 17.3 %collective-permute-start.8 = (bf16[32,5120]{1,0:T(8,128)(2,1)S(1)}, bf16[32,5120]{1,0:T(8,128)(2,1)S(1)}, u32[]{:S(2)}, u32[]{:S(2)}) collective-permute-start(bf16[32,5120]{1,0:T(8,128)(2,1)S(1)} %pad_maximum_fusion.18), channel_id=1, source_target_pairs={{0,16},{2,18},{4,20},{6,22},{8,24},{10,26},{12,28},{14,30},{16,0},... | collective-permute-start | bytes 983048 | tf_op jit(solution)/shard_map/ppermute | solution.py:1029
  48.7 8.9 %collective-permute-start.7 = (f32[2,48,128]{2,1,0:T(8,128)S(1)}, f32[2,48,128]{2,1,0:T(8,128)S(1)}, u32[]{:S(2)}, u32[]{:S(2)}) collective-permute-start(f32[2,48,128]{2,1,0:T(8,128)S(1)} %slice_bitcast_fusion.4), channel_id=1, source_target_pairs={{0,16},{2,18},{4,20},{6,22},{8,24},{10,26},{12,28},{14,30},{16,0},... | collective-permute-start | bytes 147464 | tf_op jit(solution)/shard_map/ppermute | solution.py:1029
  50.8 23.5 %collective-permute-start.10 = (bf16[2,4,32,1536]{3,2,1,0:T(8,128)(2,1)S(1)}, bf16[2,4,32,1536]{3,2,1,0:T(8,128)(2,1)S(1)}, u32[]{:S(2)}, u32[]{:S(2)}) collective-permute-start(bf16[2,4,32,1536]{3,2,1,0:T(8,128)(2,1)S(1)} %pad_maximum_fusion.5.refs_1_), channel_id=1, source_target_pairs={{0,1},{1,0},{2,3},{3,2},{4,5},{5,4},{6,7},{7,6},{8,9},{9,8},{10,11... | collective-permute-start | bytes 2359304 | tf_op jit(solution)/shard_map/ppermute | solution.py:1023
  51.6 22.7 %collective-permute-start.13 = (bf16[2,4,32,1536]{3,2,1,0:T(8,128)(2,1)S(1)}, bf16[2,4,32,1536]{3,2,1,0:T(8,128)(2,1)S(1)}, u32[]{:S(2)}, u32[]{:S(2)}) collective-permute-start(bf16[2,4,32,1536]{3,2,1,0:T(8,128)(2,1)S(1)} %pad_maximum_fusion.5.refs_1_), channel_id=1, source_target_pairs={{0,2},{2,0},{4,6},{6,4},{8,10},{10,8},{12,14},{14,12},{16,18},{18,... | collective-permute-start | bytes 2359304 | tf_op jit(solution)/shard_map/ppermute | solution.py:1029
  51.6 22.7 %collective-permute-start.12 = (bf16[2,4,32,1536]{3,2,1,0:T(8,128)(2,1)S(1)}, bf16[2,4,32,1536]{3,2,1,0:T(8,128)(2,1)S(1)}, u32[]{:S(2)}, u32[]{:S(2)}) collective-permute-start(bf16[2,4,32,1536]{3,2,1,0:T(8,128)(2,1)S(1)} %pad_maximum_fusion.4.refs_0_), channel_id=1, source_target_pairs={{0,2},{2,0},{4,6},{6,4},{8,10},{10,8},{12,14},{14,12},{16,18},{18,... | collective-permute-start | bytes 2359304 | tf_op jit(solution)/shard_map/ppermute | solution.py:1029
  56.1 18.2 %collective-permute-start.9 = (bf16[2,4,32,1536]{3,2,1,0:T(8,128)(2,1)S(1)}, bf16[2,4,32,1536]{3,2,1,0:T(8,128)(2,1)S(1)}, u32[]{:S(2)}, u32[]{:S(2)}) collective-permute-start(bf16[2,4,32,1536]{3,2,1,0:T(8,128)(2,1)S(1)} %pad_maximum_fusion.4.refs_0_), channel_id=1, source_target_pairs={{0,4},{2,6},{4,0},{6,2},{8,12},{10,14},{12,8},{14,10},{16,20},{18,... | collective-permute-start | bytes 2359304 | tf_op jit(solution)/shard_map/ppermute | solution.py:1029
  58.3 14.9 %collective-permute-start.11 = (bf16[2,32,5120]{2,1,0:T(8,128)(2,1)S(1)}, bf16[2,32,5120]{2,1,0:T(8,128)(2,1)S(1)}, u32[]{:S(2)}, u32[]{:S(2)}) collective-permute-start(bf16[2,32,5120]{2,1,0:T(8,128)(2,1)S(1)} %pad_maximum_fusion.6), channel_id=1, source_target_pairs={{0,8},{2,10},{4,12},{6,14},{8,0},{10,2},{12,4},{14,6},{16,24},{18,... | collective-permute-start | bytes 1966088 | tf_op jit(solution)/shard_map/ppermute | solution.py:1029
  74.4 7.1 %collective-permute-start.15 = (bf16[2,4,32,1536]{3,2,1,0:T(8,128)(2,1)S(1)}, bf16[2,4,32,1536]{3,2,1,0:T(8,128)(2,1)S(1)}, u32[]{:S(2)}, u32[]{:S(2)}) collective-permute-start(bf16[2,4,32,1536]{3,2,1,0:T(8,128)(2,1)S(1)} %collective-permute-done.9.refs_2_), channel_id=1, source_target_pairs={{0,2},{2,0},{4,6},{6,4},{8,10},{10,8},{12,14},{14,12},{16,18},{18,... | collective-permute-start | bytes 2359304 | tf_op jit(solution)/shard_map/ppermute | solution.py:1029
  74.5 7.9 %collective-permute-start.16 = (bf16[2,4,32,1536]{3,2,1,0:T(8,128)(2,1)S(1)}, bf16[2,4,32,1536]{3,2,1,0:T(8,128)(2,1)}, u32[]{:S(2)}, u32[]{:S(2)}) collective-permute-start(bf16[2,4,32,1536]{3,2,1,0:T(8,128)(2,1)S(1)} %collective-permute-done.10.refs_3_), channel_id=1, source_target_pairs={{0,2},{2,0},{4,6},{6,4},{8,10},{10,8},{12,14},{14,12},{16,18},{18,... | collective-permute-start | bytes 2359304 | tf_op jit(solution)/shard_map/ppermute | solution.py:1029
  77.0 16.6 %collective-permute-start.17 = (bf16[4,32,2560]{2,1,0:T(8,128)(2,1)S(1)}, bf16[4,32,2560]{2,1,0:T(8,128)(2,1)S(1)}, u32[]{:S(2)}, u32[]{:S(2)}) collective-permute-start(bf16[4,32,2560]{2,1,0:T(8,128)(2,1)S(1)} %pad_maximum_fusion.7), channel_id=1, source_target_pairs={{0,1},{1,0},{2,3},{3,2},{4,5},{5,4},{6,7},{7,6},{8,9},{9,8},{10,11... | collective-permute-start | bytes 1966088 | tf_op jit(solution)/shard_map/ppermute | solution.py:1023
  78.5 15.1 %collective-permute-start.18 = (bf16[4,32,2560]{2,1,0:T(8,128)(2,1)S(1)}, bf16[4,32,2560]{2,1,0:T(8,128)(2,1)}, u32[]{:S(2)}, u32[]{:S(2)}) collective-permute-start(bf16[4,32,2560]{2,1,0:T(8,128)(2,1)S(1)} %pad_maximum_fusion.8), channel_id=1, source_target_pairs={{0,4},{2,6},{4,0},{6,2},{8,12},{10,14},{12,8},{14,10},{16,20},{18,... | collective-permute-start | bytes 1966088 | tf_op jit(solution)/shard_map/ppermute | solution.py:1029
  97.1 16.7 %collective-permute-start.20 = (bf16[2,4,32,2560]{3,2,1,0:T(8,128)(2,1)S(1)}, bf16[2,4,32,2560]{3,2,1,0:T(8,128)(2,1)S(1)}, u32[]{:S(2)}, u32[]{:S(2)}) collective-permute-start(bf16[2,4,32,2560]{3,2,1,0:T(8,128)(2,1)S(1)} %pad_maximum_fusion.refs_0_), channel_id=1, source_target_pairs={{0,2},{2,0},{4,6},{6,4},{8,10},{10,8},{12,14},{14,12},{16,18},{18,... | collective-permute-start | bytes 3932168 | tf_op jit(solution)/shard_map/ppermute | solution.py:1029
  97.2 16.7 %collective-permute-start.21 = (bf16[2,4,32,2560]{3,2,1,0:T(8,128)(2,1)S(1)}, bf16[2,4,32,2560]{3,2,1,0:T(8,128)(2,1)S(1)}, u32[]{:S(2)}, u32[]{:S(2)}) collective-permute-start(bf16[2,4,32,2560]{3,2,1,0:T(8,128)(2,1)S(1)} %pad_maximum_fusion.1.refs_1_), channel_id=1, source_target_pairs={{0,2},{2,0},{4,6},{6,4},{8,10},{10,8},{12,14},{14,12},{16,18},{18,... | collective-permute-start | bytes 3932168 | tf_op jit(solution)/shard_map/ppermute | solution.py:1029
  97.7 40.7 %collective-permute-start.22 = (bf16[2,4,32,2560]{3,2,1,0:T(8,128)(2,1)S(1)}, bf16[2,4,32,2560]{3,2,1,0:T(8,128)(2,1)S(1)}, u32[]{:S(2)}, u32[]{:S(2)}) collective-permute-start(bf16[2,4,32,2560]{3,2,1,0:T(8,128)(2,1)S(1)} %pad_maximum_fusion.refs_0_), channel_id=1, source_target_pairs={{0,4},{2,6},{4,0},{6,2},{8,12},{10,14},{12,8},{14,10},{16,20},{18,... | collective-permute-start | bytes 3932168 | tf_op jit(solution)/shard_map/ppermute | solution.py:1029
  98.4 40.0 %collective-permute-start.23 = (bf16[2,4,32,2560]{3,2,1,0:T(8,128)(2,1)S(1)}, bf16[2,4,32,2560]{3,2,1,0:T(8,128)(2,1)S(1)}, u32[]{:S(2)}, u32[]{:S(2)}) collective-permute-start(bf16[2,4,32,2560]{3,2,1,0:T(8,128)(2,1)S(1)} %pad_maximum_fusion.1.refs_1_), channel_id=1, source_target_pairs={{0,1},{1,0},{2,3},{3,2},{4,5},{5,4},{6,7},{7,6},{8,9},{9,8},{10,11... | collective-permute-start | bytes 3932168 | tf_op jit(solution)/shard_map/ppermute | solution.py:1023
  99.0 14.9 %collective-permute-start.19 = (bf16[128,1024]{1,0:T(8,128)(2,1)S(1)}, bf16[128,1024]{1,0:T(8,128)(2,1)S(1)}, u32[]{:S(2)}, u32[]{:S(2)}) collective-permute-start(bf16[128,1024]{1,0:T(8,128)(2,1)S(1)} %convert_element_type.79), channel_id=1, source_target_pairs={{0,16},{2,18},{4,20},{6,22},{8,24},{10,26},{12,28},{14,30},{16,0},... | collective-permute-start | bytes 786440 | tf_op jit(solution)/shard_map/ppermute | solution.py:1029
  114.0 24.5 %collective-permute-start.24 = (bf16[2,128,1024]{2,1,0:T(8,128)(2,1)S(1)}, bf16[2,128,1024]{2,1,0:T(8,128)(2,1)S(1)}, u32[]{:S(2)}, u32[]{:S(2)}) collective-permute-start(bf16[2,128,1024]{2,1,0:T(8,128)(2,1)S(1)} %pad_maximum_fusion.9), channel_id=1, source_target_pairs={{0,8},{2,10},{4,12},{6,14},{8,0},{10,2},{12,4},{14,6},{16,24},{18,... | collective-permute-start | bytes 1572872 | tf_op jit(solution)/shard_map/ppermute | solution.py:1029
  139.5 4.9 %collective-permute-start.26 = (bf16[2,4,32,2560]{3,2,1,0:T(8,128)(2,1)S(1)}, bf16[2,4,32,2560]{3,2,1,0:T(8,128)(2,1)S(1)}, u32[]{:S(2)}, u32[]{:S(2)}) collective-permute-start(bf16[2,4,32,2560]{3,2,1,0:T(8,128)(2,1)S(1)} %collective-permute-done.23.refs_3_), channel_id=1, source_target_pairs={{0,2},{2,0},{4,6},{6,4},{8,10},{10,8},{12,14},{14,12},{16,18},{18,... | collective-permute-start | bytes 3932168 | tf_op jit(solution)/shard_map/ppermute | solution.py:1029
  140.2 16.3 %collective-permute-start.27 = (bf16[4,128,512]{2,1,0:T(8,128)(2,1)S(1)}, bf16[4,128,512]{2,1,0:T(8,128)(2,1)S(1)}, u32[]{:S(2)}, u32[]{:S(2)}) collective-permute-start(bf16[4,128,512]{2,1,0:T(8,128)(2,1)S(1)} %pad_maximum_fusion.10), channel_id=1, source_target_pairs={{0,1},{1,0},{2,3},{3,2},{4,5},{5,4},{6,7},{7,6},{8,9},{9,8},{10,11... | collective-permute-start | bytes 1572872 | tf_op jit(solution)/shard_map/ppermute | solution.py:1023
  141.8 14.8 %collective-permute-start.28 = (bf16[4,128,512]{2,1,0:T(8,128)(2,1)S(1)}, bf16[4,128,512]{2,1,0:T(8,128)(2,1)S(1)}, u32[]{:S(2)}, u32[]{:S(2)}) collective-permute-start(bf16[4,128,512]{2,1,0:T(8,128)(2,1)S(1)} %pad_maximum_fusion.11), channel_id=1, source_target_pairs={{0,4},{2,6},{4,0},{6,2},{8,12},{10,14},{12,8},{14,10},{16,20},{18,... | collective-permute-start | bytes 1572872 | tf_op jit(solution)/shard_map/ppermute | solution.py:1029
  158.7 26.9 %collective-permute-start.31 = (bf16[680,1024]{1,0:T(8,128)(2,1)}, bf16[680,1024]{1,0:T(8,128)(2,1)}, u32[]{:S(2)}, u32[]{:S(2)}) collective-permute-start(bf16[680,1024]{1,0:T(8,128)(2,1)} %add_convert_fusion.x_ref.refs_0_), channel_id=1, source_target_pairs={{0,2},{2,0},{4,6},{6,4},{8,10},{10,8},{12,14},{14,12},{16,18},{18,... | collective-permute-start | bytes 4177928 | tf_op jit(solution)/shard_map/ppermute | solution.py:988
  158.9 25.8 %collective-permute-start.29 = (bf16[2,4,128,512]{3,2,1,0:T(8,128)(2,1)}, bf16[2,4,128,512]{3,2,1,0:T(8,128)(2,1)}, u32[]{:S(2)}, u32[]{:S(2)}) collective-permute-start(bf16[2,4,128,512]{3,2,1,0:T(8,128)(2,1)} %pad_maximum_fusion.2.refs_0_), channel_id=1, source_target_pairs={{0,4},{2,6},{4,0},{6,2},{8,12},{10,14},{12,8},{14,10},{16,20},{18,... | collective-permute-start | bytes 3145736 | tf_op jit(solution)/shard_map/ppermute | solution.py:1029
  160.2 25.5 %collective-permute-start.30 = (bf16[2,4,128,512]{3,2,1,0:T(8,128)(2,1)}, bf16[2,4,128,512]{3,2,1,0:T(8,128)(2,1)}, u32[]{:S(2)}, u32[]{:S(2)}) collective-permute-start(bf16[2,4,128,512]{3,2,1,0:T(8,128)(2,1)} %pad_maximum_fusion.3.refs_1_), channel_id=1, source_target_pairs={{0,1},{1,0},{2,3},{3,2},{4,5},{5,4},{6,7},{7,6},{8,9},{9,8},{10,11... | collective-permute-start | bytes 3145736 | tf_op jit(solution)/shard_map/ppermute | solution.py:1023
  162.4 23.8 %collective-permute-start.32 = (bf16[2,4,128,512]{3,2,1,0:T(8,128)(2,1)}, bf16[2,4,128,512]{3,2,1,0:T(8,128)(2,1)}, u32[]{:S(2)}, u32[]{:S(2)}) collective-permute-start(bf16[2,4,128,512]{3,2,1,0:T(8,128)(2,1)} %pad_maximum_fusion.2.refs_0_), channel_id=1, source_target_pairs={{0,2},{2,0},{4,6},{6,4},{8,10},{10,8},{12,14},{14,12},{16,18},{18,... | collective-permute-start | bytes 3145736 | tf_op jit(solution)/shard_map/ppermute | solution.py:1029
  162.4 23.7 %collective-permute-start.33 = (bf16[2,4,128,512]{3,2,1,0:T(8,128)(2,1)}, bf16[2,4,128,512]{3,2,1,0:T(8,128)(2,1)}, u32[]{:S(2)}, u32[]{:S(2)}) collective-permute-start(bf16[2,4,128,512]{3,2,1,0:T(8,128)(2,1)} %pad_maximum_fusion.3.refs_1_), channel_id=1, source_target_pairs={{0,2},{2,0},{4,6},{6,4},{8,10},{10,8},{12,14},{14,12},{16,18},{18,... | collective-permute-start | bytes 3145736 | tf_op jit(solution)/shard_map/ppermute | solution.py:1029
  185.7 4.4 %collective-permute-start.35 = (bf16[2,4,128,512]{3,2,1,0:T(8,128)(2,1)}, bf16[2,4,128,512]{3,2,1,0:T(8,128)(2,1)S(1)}, u32[]{:S(2)}, u32[]{:S(2)}) collective-permute-start(bf16[2,4,128,512]{3,2,1,0:T(8,128)(2,1)} %collective-permute-done.30.refs_3_), channel_id=1, source_target_pairs={{0,2},{2,0},{4,6},{6,4},{8,10},{10,8},{12,14},{14,12},{16,18},{18,... | collective-permute-start | bytes 3145736 | tf_op jit(solution)/shard_map/ppermute | solution.py:1029
  190.0 14.5 %collective-permute-start.36 = (bf16[680,4096]{1,0:T(8,128)(2,1)}, bf16[680,4096]{1,0:T(8,128)(2,1)}, u32[]{:S(2)}, u32[]{:S(2)}) collective-permute-start(bf16[680,4096]{1,0:T(8,128)(2,1)} %get-tuple-element.612.own_ref.x_ref), channel_id=1, source_target_pairs={{0,2},{2,0},{4,6},{6,4},{8,10},{10,8},{12,14},{14,12},{16,18},{18,... | collective-permute-start | bytes 16711688 | tf_op jit(solution)/shard_map/ppermute | solution.py:988
  190.2 14.3 %collective-permute-start.38 = (bf16[680,1024]{1,0:T(8,128)(2,1)S(1)}, bf16[680,1024]{1,0:T(8,128)(2,1)}, u32[]{:S(2)}, u32[]{:S(2)}) collective-permute-start(bf16[680,1024]{1,0:T(8,128)(2,1)S(1)} %copy-done.5), channel_id=1, source_target_pairs={{0,2},{2,0},{4,6},{6,4},{8,10},{10,8},{12,14},{14,12},{16,18},{18,... | collective-permute-start | bytes 4177928 | tf_op jit(solution)/shard_map/ppermute | solution.py:988
  190.5 13.9 %collective-permute-start.39 = (bf16[680,1024]{1,0:T(8,128)(2,1)S(1)}, bf16[680,1024]{1,0:T(8,128)(2,1)}, u32[]{:S(2)}, u32[]{:S(2)}) collective-permute-start(bf16[680,1024]{1,0:T(8,128)(2,1)S(1)} %copy-done.28), channel_id=1, source_target_pairs={{0,2},{2,0},{4,6},{6,4},{8,10},{10,8},{12,14},{14,12},{16,18},{18,... | collective-permute-start | bytes 4177928 | tf_op jit(solution)/shard_map/ppermute | solution.py:988
  191.0 13.5 %collective-permute-start.37 = (bf16[680,512]{1,0:T(8,128)(2,1)}, bf16[680,512]{1,0:T(8,128)(2,1)}, u32[]{:S(2)}, u32[]{:S(2)}) collective-permute-start(bf16[680,512]{1,0:T(8,128)(2,1)} %constant_dynamic-slice_fusion), channel_id=1, source_target_pairs={{0,2},{2,0},{4,6},{6,4},{8,10},{10,8},{12,14},{14,12},{16,18},{18,... | collective-permute-start | bytes 2088968 | tf_op jit(solution)/shard_map/ppermute | solution.py:988
  204.5 38.9 %collective-permute-start.42 = (bf16[680,2048]{1,0:T(8,128)(2,1)}, bf16[680,2048]{1,0:T(8,128)(2,1)}, u32[]{:S(2)}, u32[]{:S(2)}) collective-permute-start(bf16[680,2048]{1,0:T(8,128)(2,1)} %get-tuple-element.501), channel_id=1, source_target_pairs={{0,2},{2,0},{4,6},{6,4},{8,10},{10,8},{12,14},{14,12},{16,18},{18,... | collective-permute-start | bytes 8355848 | tf_op jit(solution)/shard_map/ppermute | solution.py:988
  216.7 25.5 %collective-permute-start.40 = (bf16[2,4,2,128,256]{4,3,2,1,0:T(8,128)(2,1)}, bf16[2,4,2,128,256]{4,3,2,1,0:T(8,128)(2,1)S(1)}, u32[]{:S(2)}, u32[]{:S(2)}) collective-permute-start(bf16[2,4,2,128,256]{4,3,2,1,0:T(8,128)(2,1)} %get-tuple-element.499), channel_id=1, source_target_pairs={{0,1},{1,0},{2,3},{3,2},{4,5},{5,4},{6,7},{7,6},{8,9},{9,8},{10,11... | collective-permute-start | bytes 3145736 | tf_op jit(solution)/shard_map/ppermute | solution.py:1023
  218.2 25.2 %collective-permute-start.41 = (bf16[2,4,2,128,256]{4,3,2,1,0:T(8,128)(2,1)}, bf16[2,4,2,128,256]{4,3,2,1,0:T(8,128)(2,1)S(1)}, u32[]{:S(2)}, u32[]{:S(2)}) collective-permute-start(bf16[2,4,2,128,256]{4,3,2,1,0:T(8,128)(2,1)} %get-tuple-element.500), channel_id=1, source_target_pairs={{0,4},{2,6},{4,0},{6,2},{8,12},{10,14},{12,8},{14,10},{16,20},{18,... | collective-permute-start | bytes 3145736 | tf_op jit(solution)/shard_map/ppermute | solution.py:1029
  239.0 8.4 %collective-permute-start.43 = (bf16[680,512]{1,0:T(8,128)(2,1)S(1)}, bf16[680,512]{1,0:T(8,128)(2,1)}, u32[]{:S(2)}, u32[]{:S(2)}) collective-permute-start(bf16[680,512]{1,0:T(8,128)(2,1)S(1)} %get-tuple-element.512), channel_id=1, source_target_pairs={{0,2},{2,0},{4,6},{6,4},{8,10},{10,8},{12,14},{14,12},{16,18},{18,... | collective-permute-start | bytes 2088968 | tf_op jit(solution)/shard_map/ppermute | solution.py:988
  246.1 19.1 %collective-permute-start.44 = (bf16[4,2,128,256]{3,2,1,0:T(8,128)(2,1)}, bf16[4,2,128,256]{3,2,1,0:T(8,128)(2,1)}, u32[]{:S(2)}, u32[]{:S(2)}) collective-permute-start(bf16[4,2,128,256]{3,2,1,0:T(8,128)(2,1)} %get-tuple-element.514), channel_id=1, source_target_pairs={{0,4},{2,6},{4,0},{6,2},{8,12},{10,14},{12,8},{14,10},{16,20},{18,... | collective-permute-start | bytes 1572872 | tf_op jit(solution)/shard_map/ppermute | solution.py:1029
  246.9 18.3 %collective-permute-start.45 = (bf16[4,2,128,256]{3,2,1,0:T(8,128)(2,1)}, bf16[4,2,128,256]{3,2,1,0:T(8,128)(2,1)}, u32[]{:S(2)}, u32[]{:S(2)}) collective-permute-start(bf16[4,2,128,256]{3,2,1,0:T(8,128)(2,1)} %get-tuple-element.515), channel_id=1, source_target_pairs={{0,1},{1,0},{2,3},{3,2},{4,5},{5,4},{6,7},{7,6},{8,9},{9,8},{10,11... | collective-permute-start | bytes 1572872 | tf_op jit(solution)/shard_map/ppermute | solution.py:1023
  265.2 40.6 %collective-permute-start.47 = (bf16[2,4,2,32,1280]{4,3,2,1,0:T(8,128)(2,1)}, bf16[2,4,2,32,1280]{4,3,2,1,0:T(8,128)(2,1)S(1)}, u32[]{:S(2)}, u32[]{:S(2)}) collective-permute-start(bf16[2,4,2,32,1280]{4,3,2,1,0:T(8,128)(2,1)} %get-tuple-element.536), channel_id=1, source_target_pairs={{0,1},{1,0},{2,3},{3,2},{4,5},{5,4},{6,7},{7,6},{8,9},{9,8},{10,11... | collective-permute-start | bytes 3932168 | tf_op jit(solution)/shard_map/ppermute | solution.py:1023
  266.8 39.0 %collective-permute-start.48 = (bf16[2,4,2,32,1280]{4,3,2,1,0:T(8,128)(2,1)}, bf16[2,4,2,32,1280]{4,3,2,1,0:T(8,128)(2,1)S(1)}, u32[]{:S(2)}, u32[]{:S(2)}) collective-permute-start(bf16[2,4,2,32,1280]{4,3,2,1,0:T(8,128)(2,1)} %get-tuple-element.537), channel_id=1, source_target_pairs={{0,4},{2,6},{4,0},{6,2},{8,12},{10,14},{12,8},{14,10},{16,20},{18,... | collective-permute-start | bytes 3932168 | tf_op jit(solution)/shard_map/ppermute | solution.py:1029
  270.1 35.7 %collective-permute-start.46 = (bf16[2,2,128,512]{3,2,1,0:T(8,128)(2,1)S(1)}, bf16[2,2,128,512]{3,2,1,0:T(8,128)(2,1)S(1)}, u32[]{:S(2)}, u32[]{:S(2)}) collective-permute-start(bf16[2,2,128,512]{3,2,1,0:T(8,128)(2,1)S(1)} %get-tuple-element.535), channel_id=1, source_target_pairs={{0,8},{2,10},{4,12},{6,14},{8,0},{10,2},{12,4},{14,6},{16,24},{18,... | collective-permute-start | bytes 1572872 | tf_op jit(solution)/shard_map/ppermute | solution.py:1029
  305.8 8.8 %collective-permute-start.49 = (bf16[680,1536]{1,0:T(8,128)(2,1)S(1)}, bf16[680,1536]{1,0:T(8,128)(2,1)}, u32[]{:S(2)}, u32[]{:S(2)}) collective-permute-start(bf16[680,1536]{1,0:T(8,128)(2,1)S(1)} %get-tuple-element.558), channel_id=1, source_target_pairs={{0,2},{2,0},{4,6},{6,4},{8,10},{10,8},{12,14},{14,12},{16,18},{18,... | collective-permute-start | bytes 6266888 | tf_op jit(solution)/shard_map/ppermute | solution.py:988
  309.6 17.4 %collective-permute-start.51 = (bf16[4,2,32,1280]{3,2,1,0:T(8,128)(2,1)}, bf16[4,2,32,1280]{3,2,1,0:T(8,128)(2,1)}, u32[]{:S(2)}, u32[]{:S(2)}) collective-permute-start(bf16[4,2,32,1280]{3,2,1,0:T(8,128)(2,1)} %get-tuple-element.561), channel_id=1, source_target_pairs={{0,4},{2,6},{4,0},{6,2},{8,12},{10,14},{12,8},{14,10},{16,20},{18,... | collective-permute-start | bytes 1966088 | tf_op jit(solution)/shard_map/ppermute | solution.py:1029
  310.8 16.6 %collective-permute-start.52 = (bf16[4,2,32,1280]{3,2,1,0:T(8,128)(2,1)}, bf16[4,2,32,1280]{3,2,1,0:T(8,128)(2,1)}, u32[]{:S(2)}, u32[]{:S(2)}) collective-permute-start(bf16[4,2,32,1280]{3,2,1,0:T(8,128)(2,1)} %get-tuple-element.562), channel_id=1, source_target_pairs={{0,1},{1,0},{2,3},{3,2},{4,5},{5,4},{6,7},{7,6},{8,9},{9,8},{10,11... | collective-permute-start | bytes 1966088 | tf_op jit(solution)/shard_map/ppermute | solution.py:1023
  312.7 14.3 %collective-permute-start.50 = (bf16[2,128,512]{2,1,0:T(8,128)(2,1)}, bf16[2,128,512]{2,1,0:T(8,128)(2,1)S(1)}, u32[]{:S(2)}, u32[]{:S(2)}) collective-permute-start(bf16[2,128,512]{2,1,0:T(8,128)(2,1)} %bitcast.44), channel_id=1, source_target_pairs={{0,16},{2,18},{4,20},{6,22},{8,24},{10,26},{12,28},{14,30},{16,0},... | collective-permute-start | bytes 786440 | tf_op jit(solution)/shard_map/ppermute | solution.py:1029
  327.4 24.3 %collective-permute-start.53 = (bf16[2,4,2,32,768]{4,3,2,1,0:T(8,128)(2,1)}, bf16[2,4,2,32,768]{4,3,2,1,0:T(8,128)(2,1)S(1)}, u32[]{:S(2)}, u32[]{:S(2)}) collective-permute-start(bf16[2,4,2,32,768]{4,3,2,1,0:T(8,128)(2,1)} %get-tuple-element.590), channel_id=1, source_target_pairs={{0,1},{1,0},{2,3},{3,2},{4,5},{5,4},{6,7},{7,6},{8,9},{9,8},{10,11... | collective-permute-start | bytes 2359304 | tf_op jit(solution)/shard_map/ppermute | solution.py:1023
  328.6 23.2 %collective-permute-start.54 = (bf16[2,4,2,32,768]{4,3,2,1,0:T(8,128)(2,1)}, bf16[2,4,2,32,768]{4,3,2,1,0:T(8,128)(2,1)S(1)}, u32[]{:S(2)}, u32[]{:S(2)}) collective-permute-start(bf16[2,4,2,32,768]{4,3,2,1,0:T(8,128)(2,1)} %get-tuple-element.591), channel_id=1, source_target_pairs={{0,4},{2,6},{4,0},{6,2},{8,12},{10,14},{12,8},{14,10},{16,20},{18,... | collective-permute-start | bytes 2359304 | tf_op jit(solution)/shard_map/ppermute | solution.py:1029
  332.7 19.1 %collective-permute-start.55 = (bf16[2,2,32,2560]{3,2,1,0:T(8,128)(2,1)S(1)}, bf16[2,2,32,2560]{3,2,1,0:T(8,128)(2,1)S(1)}, u32[]{:S(2)}, u32[]{:S(2)}) collective-permute-start(bf16[2,2,32,2560]{3,2,1,0:T(8,128)(2,1)S(1)} %get-tuple-element.592), channel_id=1, source_target_pairs={{0,8},{2,10},{4,12},{6,14},{8,0},{10,2},{12,4},{14,6},{16,24},{18,... | collective-permute-start | bytes 1966088 | tf_op jit(solution)/shard_map/ppermute | solution.py:1029
  352.9 19.0 %collective-permute-start.56 = (bf16[4,2,32,768]{3,2,1,0:T(8,128)(2,1)S(1)}, bf16[4,2,32,768]{3,2,1,0:T(8,128)(2,1)S(1)}, u32[]{:S(2)}, u32[]{:S(2)}) collective-permute-start(bf16[4,2,32,768]{3,2,1,0:T(8,128)(2,1)S(1)} %get-tuple-element.609), channel_id=1, source_target_pairs={{0,4},{2,6},{4,0},{6,2},{8,12},{10,14},{12,8},{14,10},{16,20},{18,... | collective-permute-start | bytes 1179656 | tf_op jit(solution)/shard_map/ppermute | solution.py:1029
  354.0 18.0 %collective-permute-start.57 = (bf16[4,2,32,768]{3,2,1,0:T(8,128)(2,1)S(1)}, bf16[4,2,32,768]{3,2,1,0:T(8,128)(2,1)S(1)}, u32[]{:S(2)}, u32[]{:S(2)}) collective-permute-start(bf16[4,2,32,768]{3,2,1,0:T(8,128)(2,1)S(1)} %get-tuple-element.610), channel_id=1, source_target_pairs={{0,1},{1,0},{2,3},{3,2},{4,5},{5,4},{6,7},{7,6},{8,9},{9,8},{10,11... | collective-permute-start | bytes 1179656 | tf_op jit(solution)/shard_map/ppermute | solution.py:1023
  355.7 16.2 %collective-permute-start.58 = (bf16[2,32,2560]{2,1,0:T(8,128)(2,1)S(1)}, bf16[2,32,2560]{2,1,0:T(8,128)(2,1)S(1)}, u32[]{:S(2)}, u32[]{:S(2)}) collective-permute-start(bf16[2,32,2560]{2,1,0:T(8,128)(2,1)S(1)} %bitcast.126), channel_id=1, source_target_pairs={{0,16},{2,18},{4,20},{6,22},{8,24},{10,26},{12,28},{14,30},{16,0},... | collective-permute-start | bytes 983048 | tf_op jit(solution)/shard_map/ppermute | solution.py:1029
  359.0 28.3 %collective-permute-start.61 = (f32[128,512]{1,0:T(8,128)}, f32[128,512]{1,0:T(8,128)}, u32[]{:S(2)}, u32[]{:S(2)}) collective-permute-start(f32[128,512]{1,0:T(8,128)} %bitcast.52), channel_id=1, source_target_pairs={{0,2},{2,0},{4,6},{6,4},{8,10},{10,8},{12,14},{14,12},{16,18},{18,... | collective-permute-start | bytes 786440 | tf_op jit(solution)/shard_map/ppermute | solution.py:1029
  374.1 11.5 %collective-permute-start.59 = (bf16[2,2,32,1536]{3,2,1,0:T(8,128)(2,1)S(1)}, bf16[2,2,32,1536]{3,2,1,0:T(8,128)(2,1)S(1)}, u32[]{:S(2)}, u32[]{:S(2)}) collective-permute-start(bf16[2,2,32,1536]{3,2,1,0:T(8,128)(2,1)S(1)} %get-tuple-element.633), channel_id=1, source_target_pairs={{0,8},{2,10},{4,12},{6,14},{8,0},{10,2},{12,4},{14,6},{16,24},{18,... | collective-permute-start | bytes 1179656 | tf_op jit(solution)/shard_map/ppermute | solution.py:1029
  374.1 13.2 %collective-permute-start.62 = (f32[32,2560]{1,0:T(8,128)}, f32[32,2560]{1,0:T(8,128)}, u32[]{:S(2)}, u32[]{:S(2)}) collective-permute-start(f32[32,2560]{1,0:T(8,128)} %bitcast.54), channel_id=1, source_target_pairs={{0,2},{2,0},{4,6},{6,4},{8,10},{10,8},{12,14},{14,12},{16,18},{18,... | collective-permute-start | bytes 983048 | tf_op jit(solution)/shard_map/ppermute | solution.py:1029
  385.6 8.3 %collective-permute-start.64 = (bf16[2,48,128]{2,1,0:T(8,128)(2,1)S(1)}, bf16[2,48,128]{2,1,0:T(8,128)(2,1)S(1)}, u32[]{:S(2)}, u32[]{:S(2)}) collective-permute-start(bf16[2,48,128]{2,1,0:T(8,128)(2,1)S(1)} %pad_maximum_fusion.23), channel_id=1, source_target_pairs={{0,4},{2,6},{4,0},{6,2},{8,12},{10,14},{12,8},{14,10},{16,20},{18,... | collective-permute-start | bytes 73736 | tf_op jit(solution)/shard_map/ppermute | solution.py:1029
  387.3 11.3 %collective-permute-start.63 = (bf16[2,32,1536]{2,1,0:T(8,128)(2,1)S(1)}, bf16[2,32,1536]{2,1,0:T(8,128)(2,1)S(1)}, u32[]{:S(2)}, u32[]{:S(2)}) collective-permute-start(bf16[2,32,1536]{2,1,0:T(8,128)(2,1)S(1)} %bitcast.127), channel_id=1, source_target_pairs={{0,16},{2,18},{4,20},{6,22},{8,24},{10,26},{12,28},{14,30},{16,0},... | collective-permute-start | bytes 589832 | tf_op jit(solution)/shard_map/ppermute | solution.py:1029
  399.6 8.8 %collective-permute-start.65 = (f32[32,1536]{1,0:T(8,128)S(1)}, f32[32,1536]{1,0:T(8,128)S(1)}, u32[]{:S(2)}, u32[]{:S(2)}) collective-permute-start(f32[32,1536]{1,0:T(8,128)S(1)} %bitcast.128), channel_id=1, source_target_pairs={{0,2},{2,0},{4,6},{6,4},{8,10},{10,8},{12,14},{14,12},{16,18},{18,... | collective-permute-start | bytes 589832 | tf_op jit(solution)/shard_map/ppermute | solution.py:1029
  402.7 5.6 %collective-permute-start.67 = (bf16[2,2,2,48,128]{4,3,2,1,0:T(8,128)(2,1)S(1)}, bf16[2,2,2,48,128]{4,3,2,1,0:T(8,128)(2,1)S(1)}, u32[]{:S(2)}, u32[]{:S(2)}) collective-permute-start(bf16[2,2,2,48,128]{4,3,2,1,0:T(8,128)(2,1)S(1)} %get-tuple-element.723), channel_id=1, source_target_pairs={{0,16},{2,18},{4,20},{6,22},{8,24},{10,26},{12,28},{14,30},{16,0},... | collective-permute-start | bytes 294920 | tf_op jit(solution)/shard_map/ppermute | solution.py:1029
  408.3 5.7 %collective-permute-start.68 = (bf16[2,2,2,2,48,128]{5,4,3,2,1,0:T(8,128)(2,1)S(1)}, bf16[2,2,2,2,48,128]{5,4,3,2,1,0:T(8,128)(2,1)S(1)}, u32[]{:S(2)}, u32[]{:S(2)}) collective-permute-start(bf16[2,2,2,2,48,128]{5,4,3,2,1,0:T(8,128)(2,1)S(1)} %get-tuple-element.721), channel_id=1, source_target_pairs={{0,8},{2,10},{4,12},{6,14},{8,0},{10,2},{12,4},{14,6},{16,24},{18,... | collective-permute-start | bytes 589832 | tf_op jit(solution)/shard_map/ppermute | solution.py:1029
  (75 other events, 700.3 us)
